TPU v7x, 128 devices: a whole 4x4x4 slice. The times are simulated.
128 devices in a mesh: frame: 8 (over y, z_hi), strip: 16 (over z_lo, x, core).
Axes of the slice: x: 4, y: 4, z: 4 (z_hi: 2, z_lo: 2; z = z_hi * 2 + z_lo), core: 2. Of those that a mesh axis runs over, the one named last changes fastest.
Arguments:
- queries: bfloat16 [32, 1024, 3072], P('frame', 'strip'), may hold values from -96 to 96
- key_states: bfloat16 [32, 1024, 3072], P('frame', 'strip'), may hold values from -4 to 4
- value_states: bfloat16 [32, 1024, 3072], P('frame', 'strip'), may hold values from -6 to 6
- block_masks: int32 [4, 8, 8], replicated, may hold values from 0 to 1, as said below
- head_pattern: int32 [16], replicated, may hold values from 0 to 3
Outputs:
- attended: bfloat16 [32, 1024, 3072], P('frame', 'strip')
Inputs may be any that keep to these rules, and one draw needn't show every extreme that they name: Every pattern reads its diagonal block pairs: block_masks[p, b, b] = 1 for all p and b.
All inputs are finite; a program needn't handle non-finite values.
Results may differ from a plain program's by a relative error of at most 0.0046.
Values may be sent and summed in bfloat16 or wider, within the bound.
No kernel may reach another device: no remote copies, remote signals or barrier semaphores. Data moves between devices by JAX's collectives and lax.ppermute only.
A program may use at most 192 MiB of HBM per device.

v0:
```python
import math

import jax
import jax.numpy as jnp
from jax import lax
from jax.experimental import pallas as pl
from jax.experimental.pallas import tpu as pltpu
from jax.sharding import PartitionSpec as P


DH = 128
HS = 16
HT = 8
BLK = 128
NF = 8
NS = 16
QT = 512
QS = 256

NEG_FILL = -1e30
RATE = math.log2(math.e) / math.sqrt(DH)


BF16 = jnp.bfloat16
F32 = jnp.float32


def whole():
    return pl.BlockSpec(memory_space=pltpu.VMEM)


def scalars():
    return pl.BlockSpec(memory_space=pltpu.SMEM)


def anywhere():
    return pl.BlockSpec(memory_space=pl.ANY)


def in_vmem(block):
    return pltpu.with_memory_space_constraint(block, pltpu.VMEM)


def in_hbm(block):
    return pltpu.with_memory_space_constraint(block, pltpu.HBM)


def params(mib=8):
    return pltpu.CompilerParams(vmem_limit_bytes=mib * 1024 * 1024)


def split_spatial_kernel(q_ref, k_ref, v_ref, out_ref, sem):
    copies = []
    for head in range(HS):
        for part, ref in enumerate((q_ref, k_ref, v_ref)):
            copies.append(
                pltpu.make_async_copy(
                    ref.at[:, :, head * DH : (head + 1) * DH],
                    out_ref.at[head, part],
                    sem.at[len(copies)],
                )
            )
            copies[-1].start()
    for copy in copies:
        copy.wait()


def split_spatial(queries, keys, values):
    frames, spots, _ = queries.shape
    return pl.pallas_call(
        split_spatial_kernel,
        in_specs=[anywhere()] * 3,
        out_specs=whole(),
        out_shape=pltpu.VMEM((HS, 3, frames, spots, DH), BF16),
        scratch_shapes=[pltpu.SemaphoreType.DMA((HS * 3,))],
        compiler_params=params(),
        name="split_spatial",
    )(in_hbm(queries), in_hbm(keys), in_hbm(values))


def split_temporal_kernel(group_ref, q_ref, k_ref, v_ref, *rest):
    out_refs, sem = rest[:NF], rest[NF]
    group = group_ref[0]
    copies = []
    for slot in range(NF):
        at = pl.multiple_of((HS + lax.bitwise_xor(group, slot)) * DH, DH)
        for part, ref in enumerate((q_ref, k_ref, v_ref)):
            copies.append(
                pltpu.make_async_copy(
                    ref.at[:, :, pl.ds(at, DH)], out_refs[slot].at[part], sem.at[len(copies)]
                )
            )
            copies[-1].start()
    for copy in copies:
        copy.wait()


def split_temporal(group, queries, keys, values):
    frames, spots, _ = queries.shape
    return pl.pallas_call(
        split_temporal_kernel,
        in_specs=[scalars()] + [anywhere()] * 3,
        out_specs=[whole()] * NF,
        out_shape=[pltpu.VMEM((3, frames, spots, DH), BF16)] * NF,
        scratch_shapes=[pltpu.SemaphoreType.DMA((NF * 3,))],
        compiler_params=params(),
        name="split_temporal",
    )(group, in_hbm(queries), in_hbm(keys), in_hbm(values))


def collect_kernel(*refs):
    slabs, q_ref, kv_ref = refs[:NF], refs[NF], refs[NF + 1]
    per = q_ref.shape[0] // NF
    for slot in range(NF):
        at = slice(slot * per, (slot + 1) * per)
        q_ref[at] = slabs[slot][0].reshape(per, DH)
        kv_ref[0, at] = slabs[slot][1].reshape(per, DH)
        kv_ref[1, at] = slabs[slot][2].reshape(per, DH)


def collect(slabs):
    _, frames, spots, _ = slabs[0].shape
    rows = NF * frames * spots
    return pl.pallas_call(
        collect_kernel,
        in_specs=[whole()] * NF,
        out_specs=[whole()] * 2,
        out_shape=[pltpu.HBM((rows, DH), BF16), pltpu.VMEM((2, rows, DH), BF16)],
        compiler_params=params(),
        name="collect",
    )(*[in_vmem(slab) for slab in slabs])


def scores_of(q, k):
    return lax.dot_general(q, k, (((1,), (1,)), ((), ())), preferred_element_type=F32)


def with_ones(v):
    return jnp.concatenate([v, jnp.ones_like(v)], axis=1)


def temporal_kernel(offsets, resume, finish, *refs):
    count = len(offsets)
    strip_ref, q_ref = refs[:2]
    kv_refs = refs[2 : 2 + count]
    rest = list(refs[2 + count :])
    if resume:
        old_top, old_mix = rest[:2]
        rest = rest[2:]
    if finish:
        group_ref, out_ref = rest[:2]
        rest = rest[2:]
    top_ref, mix_ref, s_buf = rest[:3]
    rows = q_ref.shape[0]
    tiles = rows // QT
    own_strip = strip_ref[0]
    step = 1 - 2 * lax.rem(own_strip, 2)

    if resume:
        sem = rest[-1]
        loads = [
            pltpu.make_async_copy(old_top, top_ref, sem.at[0]),
            pltpu.make_async_copy(old_mix, mix_ref, sem.at[1]),
        ]
        for load in loads:
            load.start()
        for load in loads:
            load.wait()
    else:
        top_ref[...] = jnp.full(top_ref.shape, NEG_FILL, F32)
        mix_ref[...] = jnp.zeros(mix_ref.shape, F32)

    def attend(kv_ref):
        k = kv_ref[0]

        def q_tile(i):
            return q_ref[i * QT : (i + 1) * QT]

        s_buf[0] = scores_of(q_tile(0), k)
        for i in range(tiles):
            if i + 1 < tiles:
                s_buf[(i + 1) % 2] = scores_of(q_tile(i + 1), k)
            at = slice(i * QT, (i + 1) * QT)
            s = s_buf[i % 2]
            before = top_ref[at]
            top = jnp.maximum(before, jnp.max(s, axis=1, keepdims=True))
            fade = jnp.exp2((before - top) * RATE)
            weights = jnp.exp2((s - top[:, :1]) * RATE).astype(BF16)
            mixed = jnp.dot(weights, with_ones(kv_ref[1]), preferred_element_type=F32)
            mix_ref[at] = mixed + mix_ref[at] * jnp.concatenate([fade, fade], axis=1)
            top_ref[at] = top

    def usable(index):
        source = own_strip + offsets[index] * step
        return (source >= 0) & (source < NS)

    if count == 1:
        pl.when(usable(0))(lambda: attend(kv_refs[0]))
    else:
        kv_buf = rest[3]

        def strip(index, carry):
            valid = False
            for i in range(count):
                here = index == i

                @pl.when(here)
                def _(i=i):
                    kv_buf[...] = kv_refs[i][...]

                valid = valid | (here & usable(i))
            pl.when(valid)(lambda: attend(kv_buf))
            return carry

        lax.fori_loop(0, count, strip, 0)
    if finish:
        per = rows // NF
        for slot in range(NF):
            at = slice(slot * per, (slot + 1) * per)
            result = (mix_ref[at, :DH] / mix_ref[at, DH:]).astype(BF16)
            out_ref[lax.bitwise_xor(group_ref[0], slot)] = result.reshape(out_ref.shape[1:])


def temporal(strip, q, strips, state=None, keep=False, finish=None):
    rows = q.shape[0]
    count = len(strips)
    state_shape = [pltpu.VMEM((rows, DH), F32), pltpu.VMEM((rows, 2 * DH), F32)]
    args = [strip, in_hbm(q), *[in_vmem(x) for x in strips.values()]]
    in_specs = [scalars()] + [whole()] * (1 + count)
    scratch = [pltpu.VMEM((2, QT, rows), F32)]
    if count > 1:
        scratch.append(pltpu.VMEM((2, rows, DH), BF16))
    if state is not None:
        args += state
        in_specs += [anywhere()] * 2
        scratch.append(pltpu.SemaphoreType.DMA((2,)))
    if finish is not None:
        group, shape = finish
        args.append(group)
        in_specs.append(scalars())
        out_shape = [pltpu.HBM(shape, BF16)]
        scratch = state_shape + scratch
    elif keep:
        out_shape = state_shape
    else:
        out_shape = [pltpu.HBM(x.shape, x.dtype) for x in state_shape]
    cost = pl.CostEstimate(
        flops=count * rows**2 * DH * 8,
        transcendentals=count * rows**2,
        bytes_accessed=count * rows * DH * 4,
    )
    offsets = tuple(strips)
    return pl.pallas_call(
        lambda *refs: temporal_kernel(offsets, state is not None, finish is not None, *refs),
        in_specs=in_specs,
        out_specs=[whole()] * len(out_shape),
        out_shape=out_shape,
        scratch_shapes=scratch,
        compiler_params=params(20),
        cost_estimate=cost,
    )(*args)


def pick_kernel(strip_ref, pattern_ref, masks_ref, out_ref):
    pattern = pattern_ref[strip_ref[0]]
    blocks = out_ref.shape[0]
    for i in range(blocks):
        for j in range(blocks):
            out_ref[i, j] = masks_ref[pattern, i, j]


def pick(strip, head_pattern, masks):
    return pl.pallas_call(
        pick_kernel,
        in_specs=[scalars()] * 3,
        out_specs=scalars(),
        out_shape=jax.ShapeDtypeStruct(masks.shape[1:], masks.dtype),
        name="pick",
    )(strip, head_pattern, masks)


def spatial_kernel(mask_ref, qkv_ref, out_ref, s_buf, result_ref, sem):
    strips, frames, spots, _ = out_ref.shape
    positions = strips * spots
    blocks = positions // BLK
    tiles = positions // QS
    per = QS // spots

    def raw(f, i):
        q = qkv_ref[i * per : (i + 1) * per, 0, f].reshape(QS, DH)
        return scores_of(q, qkv_ref[:, 1, f].reshape(positions, DH))

    def masked(s, i):
        rows = []
        for r in range(QS // BLK):
            row = i * (QS // BLK) + r
            cells = []
            for j in range(blocks):
                bias = jnp.where(mask_ref[row, j] > 0, 0.0, NEG_FILL)
                cells.append(s[r * BLK : (r + 1) * BLK, j * BLK : (j + 1) * BLK] + bias)
            rows.append(jnp.concatenate(cells, axis=1))
        return jnp.concatenate(rows, axis=0)

    s_buf[0] = raw(0, 0)

    def frame(f, carry):
        v = with_ones(qkv_ref[:, 2, f].reshape(positions, DH))
        for i in range(tiles):
            if i + 1 < tiles:
                s_buf[(i + 1) % 2] = raw(f, i + 1)
            else:
                s_buf[(i + 1) % 2] = raw(jnp.minimum(f + 1, frames - 1), 0)
            s = masked(s_buf[i % 2], i)
            top = jnp.max(s, axis=1, keepdims=True)
            weights = jnp.exp2((s - top) * RATE).astype(BF16)
            mixed = jnp.dot(weights, v, preferred_element_type=F32)
            result = (mixed[:, :DH] / mixed[:, DH:]).astype(BF16)
            result_ref[f, i * per : (i + 1) * per] = result.reshape(per, spots, DH)
        leave(f).start()
        return carry

    def leave(f):
        return pltpu.make_async_copy(result_ref.at[f], out_ref.at[:, f], sem.at[f])

    lax.fori_loop(0, frames, frame, 0)
    for f in range(frames):
        leave(f).wait()


def spatial(mask, qkv):
    strips, _, frames, spots, _ = qkv.shape
    positions = strips * spots
    cost = pl.CostEstimate(
        flops=frames * positions**2 * DH * 8,
        transcendentals=frames * positions**2,
        bytes_accessed=4 * strips * frames * spots * DH * 2,
    )
    return pl.pallas_call(
        spatial_kernel,
        in_specs=[scalars(), whole()],
        out_specs=anywhere(),
        scratch_shapes=[
            pltpu.VMEM((2, QS, positions), F32),
            pltpu.VMEM((frames, strips, spots, DH), BF16),
            pltpu.SemaphoreType.DMA((frames,)),
        ],
        out_shape=pltpu.HBM((strips, frames, spots, DH), BF16),
        compiler_params=params(12),
        cost_estimate=cost,
        name="spatial",
    )(mask, in_vmem(qkv))


def join_kernel(first, heads_ref, *rest):
    out_ref, sem = rest[-2:]
    copies = []
    for head in range(heads_ref.shape[0]):
        at = (first + head) * DH
        copies.append(
            pltpu.make_async_copy(heads_ref.at[head], out_ref.at[:, :, at : at + DH], sem.at[head])
        )
        copies[-1].start()
    for copy in copies:
        copy.wait()


def join(heads, first, partial=None):
    count, frames, spots, _ = heads.shape
    args = [in_vmem(heads)]
    if partial is not None:
        args.append(partial)
    return pl.pallas_call(
        lambda *refs: join_kernel(first, *refs),
        in_specs=[whole(), anywhere()][: len(args)],
        out_specs=anywhere(),
        out_shape=jax.ShapeDtypeStruct((frames, spots, (HS + HT) * DH), BF16),
        scratch_shapes=[pltpu.SemaphoreType.DMA((count,))],
        input_output_aliases={} if partial is None else {1: 0},
        compiler_params=params(),
        name="join_spatial" if partial is None else "join_temporal",
    )(*args)


def paired(block, slot):
    return lax.ppermute(block, "frame", [(i, i ^ slot) for i in range(NF)])


def main(queries, keys, values, block_masks, head_pattern):
    frames, spots, _ = queries.shape
    group = lax.axis_index("frame").astype(jnp.int32)
    strip = lax.axis_index("strip").astype(jnp.int32)
    group_arg = group.reshape(1)
    strip_arg = strip.reshape(1)

    slabs = split_temporal(group_arg, queries, keys, values)
    slabs = [slabs[0]] + [paired(slabs[d], d) for d in range(1, NF)]
    qkv = split_spatial(queries, keys, values)
    qkv = lax.all_to_all(qkv, "strip", split_axis=0, concat_axis=0, tiled=True)
    mask = pick(strip_arg, head_pattern, block_masks)
    t_q, own = collect(slabs)

    swap = [(i, i ^ 1) for i in range(NS)]
    shared_from = [i + 2 if i % 2 == 0 else i - 2 for i in range(NS)]
    single_from = [i - 2 if i % 2 == 0 else i + 2 for i in range(NS)]
    partner = lax.ppermute(own, "strip", swap)
    shared = lax.ppermute(
        own, "strip", [(s, i) for i, s in enumerate(shared_from) if 0 <= s < NS]
    )
    own_later, shared = lax.optimization_barrier((own, shared))
    single = lax.ppermute(
        own_later, "strip", [(s, i) for i, s in enumerate(single_from) if 0 <= s < NS]
    )
    passed = lax.ppermute(shared, "strip", swap)

    state = temporal(strip_arg, t_q, {0: own, 1: partner})
    state = temporal(strip_arg, t_q, {2: shared, -1: passed}, [in_hbm(x) for x in state], keep=True)
    t_out = temporal(
        strip_arg,
        t_q,
        {-2: single},
        [in_vmem(x) for x in state],
        finish=(group_arg, (NF, frames, spots, DH)),
    )[0]
    t_out = lax.all_to_all(t_out, "frame", split_axis=0, concat_axis=0, tiled=True)
    s_out = spatial(mask, qkv)
    s_out = lax.all_to_all(s_out, "strip", split_axis=0, concat_axis=0, tiled=True)
    partial = join(s_out, 0)
    return join(t_out, HS, partial)


def solution(mesh):
    spec = P("frame", "strip", None)
    return jax.shard_map(
        main,
        mesh=mesh,
        in_specs=(spec, spec, spec, P(), P()),
        out_specs=spec,
        check_vma=False,
    )
```

profile of v0, /device:TPU:32, one launch (start us, length us, event | category | flops | bytes accessed | tf_op | source)
XLA Modules:
  0.0 161.9 jit_solution(7857773869744027828)
XLA Ops:
  0.0 4.0 %split_spatial.1 = bf16[16,3,4,64,128]{4,3,2,1,0:T(8,128)(2,1)} custom-call(bf16[4,64,3072]{2,1,0:T(8,128)(2,1)} %q_ref.3, bf16[4,64,3072]{2,1,0:T(8,128)(2,1)} %k_ref.3, bf16[4,64,3072]{2,1,0:T(8,128)(2,1)} %v_ref.3), custom_call_target="tpu_custom_call" | custom-call | tf_op jit(solution)/shard_map/split_spatial/pallas_call | solution.py:70
  4.0 5.8 %all-to-all-start.1 = ((bf16[16,3,4,64,128]{4,3,2,1,0:T(8,128)(2,1)}), bf16[16,3,4,64,128]{4,3,2,1,0:T(8,128)(2,1)S(1)}, u32[]{:S(2)}, u32[]{:S(2)}) async-start(bf16[16,3,4,64,128]{4,3,2,1,0:T(8,128)(2,1)} %split_spatial.1), calls=%async_computation.1 | async-start | bytes 6291456 | tf_op jit(solution)/shard_map/all_to_all | solution.py:398
  9.8 1.7 %split_temporal.1 = (bf16[3,4,64,128]{3,2,1,0:T(8,128)(2,1)S(1)}, bf16[3,4,64,128]{3,2,1,0:T(8,128)(2,1)S(1)}, bf16[3,4,64,128]{3,2,1,0:T(8,128)(2,1)S(1)}, bf16...) custom-call(s32[1]{0:T(128)} %bitcast.1.group_ref.refs_5_, ...), custom_call_target="tpu_custom_call" | custom-call | tf_op jit(solution)/shard_map/split_temporal/pallas_call | solution.py:100
  11.5 3.1 %collective-permute-start = (bf16[3,4,64,128]{3,2,1,0:T(8,128)(2,1)S(1)}, bf16[3,4,64,128]{3,2,1,0:T(8,128)(2,1)S(1)}, u32[]{:S(2)}, u32[]{:S(2)}) collective-permute-start(bf16[3,4,64,128]{3,2,1,0:T(8,128)(2,1)S(1)} %get-tuple-element.22), channel_id=1, source_target_pairs={{0,16},{16,0},{32,48},{48,32},{64,80},{80,64},{96,112},{112,96},{1... | collective-permute-start | bytes 589832 | tf_op jit(solution)/shard_map/ppermute | solution.py:385
  14.6 1.6 collective-permute-start.1
  16.6 3.2 %collective-permute-start.3 = (bf16[3,4,64,128]{3,2,1,0:T(8,128)(2,1)S(1)}, bf16[3,4,64,128]{3,2,1,0:T(8,128)(2,1)S(1)}, u32[]{:S(2)}, u32[]{:S(2)}) collective-permute-start(bf16[3,4,64,128]{3,2,1,0:T(8,128)(2,1)S(1)} %get-tuple-element.25), channel_id=1, source_target_pairs={{0,64},{16,80},{32,96},{48,112},{64,0},{80,16},{96,32},{112,48},{1... | collective-permute-start | bytes 589832 | tf_op jit(solution)/shard_map/ppermute | solution.py:385
  19.8 2.7 %collective-permute-start.4 = (bf16[3,4,64,128]{3,2,1,0:T(8,128)(2,1)S(1)}, bf16[3,4,64,128]{3,2,1,0:T(8,128)(2,1)S(1)}, u32[]{:S(2)}, u32[]{:S(2)}) collective-permute-start(bf16[3,4,64,128]{3,2,1,0:T(8,128)(2,1)S(1)} %get-tuple-element.26), channel_id=1, source_target_pairs={{0,80},{16,64},{32,112},{48,96},{64,16},{80,0},{96,48},{112,32},{1... | collective-permute-start | bytes 589832 | tf_op jit(solution)/shard_map/ppermute | solution.py:385
  22.5 37.8 %collective-permute-done.refs_1_ = bf16[3,4,64,128]{3,2,1,0:T(8,128)(2,1)S(1)} collective-permute-done((bf16[3,4,64,128]{3,2,1,0:T(8,128)(2,1)S(1)}, bf16[3,4,64,128]{3,2,1,0:T(8,128)(2,1)S(1)}, u32[]{:S(2)}, u32[]{:S(2)}) %collective-permute-start) | collective-permute-done | bytes 196640 | tf_op jit(solution)/shard_map/ppermute | solution.py:385
  60.3 3.0 %collective-permute-start.5 = (bf16[3,4,64,128]{3,2,1,0:T(8,128)(2,1)S(1)}, bf16[3,4,64,128]{3,2,1,0:T(8,128)(2,1)S(1)}, u32[]{:S(2)}, u32[]{:S(2)}) collective-permute-start(bf16[3,4,64,128]{3,2,1,0:T(8,128)(2,1)S(1)} %get-tuple-element.27), channel_id=1, source_target_pairs={{0,96},{16,112},{32,64},{48,80},{64,32},{80,48},{96,0},{112,16},{1... | collective-permute-start | bytes 589832 | tf_op jit(solution)/shard_map/ppermute | solution.py:385
  63.6 5.7 %collective-permute-done.5.refs_6_ = bf16[3,4,64,128]{3,2,1,0:T(8,128)(2,1)S(1)} collective-permute-done((bf16[3,4,64,128]{3,2,1,0:T(8,128)(2,1)S(1)}, bf16[3,4,64,128]{3,2,1,0:T(8,128)(2,1)S(1)}, u32[]{:S(2)}, u32[]{:S(2)}) %collective-permute-start.5) | collective-permute-done | bytes 196640 | tf_op jit(solution)/shard_map/ppermute | solution.py:385
  69.3 3.7 %collective-permute-done.6.refs_7_ = bf16[3,4,64,128]{3,2,1,0:T(8,128)(2,1)S(1)} collective-permute-done((bf16[3,4,64,128]{3,2,1,0:T(8,128)(2,1)S(1)}, bf16[3,4,64,128]{3,2,1,0:T(8,128)(2,1)S(1)}, u32[]{:S(2)}, u32[]{:S(2)}) %collective-permute-start.6) | collective-permute-done | bytes 196640 | tf_op jit(solution)/shard_map/ppermute | solution.py:385
  73.0 1.2 collect.1
  74.3 5.2 %collective-permute-start.7 = (bf16[2,2048,128]{2,1,0:T(8,128)(2,1)}, bf16[2,2048,128]{2,1,0:T(8,128)(2,1)}, u32[]{:S(2)}, u32[]{:S(2)}) collective-permute-start(bf16[2,2048,128]{2,1,0:T(8,128)(2,1)} %get-tuple-element.31.refs_2_), channel_id=1, source_target_pairs={{2,0},{4,2},{1,3},{6,4},{3,5},{8,6},{5,7},{10,8},{7,9},{12,10},{9,... | collective-permute-start | bytes 3145736 | tf_op jit(solution)/shard_map/ppermute | solution.py:406
  79.6 1.6 pick.1.mask_ref
  81.2 10.9 %collective-permute-done.7.refs_2_ = bf16[2,2048,128]{2,1,0:T(8,128)(2,1)} collective-permute-done((bf16[2,2048,128]{2,1,0:T(8,128)(2,1)}, bf16[2,2048,128]{2,1,0:T(8,128)(2,1)}, u32[]{:S(2)}, u32[]{:S(2)}) %collective-permute-start.7) | collective-permute-done | bytes 1048608 | tf_op jit(solution)/shard_map/ppermute | solution.py:406
  92.1 2.6 %collective-permute-start.8 = (bf16[2,2048,128]{2,1,0:T(8,128)(2,1)}, bf16[2,2048,128]{2,1,0:T(8,128)(2,1)}, u32[]{:S(2)}, u32[]{:S(2)}) collective-permute-start(bf16[2,2048,128]{2,1,0:T(8,128)(2,1)} %get-tuple-element.31.refs_2_), channel_id=1, source_target_pairs={{3,1},{0,2},{5,3},{2,4},{7,5},{4,6},{9,7},{6,8},{11,9},{8,10},{13,... | collective-permute-start | bytes 3145736 | tf_op jit(solution)/shard_map/ppermute | solution.py:410
  94.8 13.8 %shard_map.55 = (f32[2048,128]{1,0:T(8,128)}, f32[2048,256]{1,0:T(8,128)}) custom-call(s32[1]{0:T(128)} %bitcast.refs_0_.strip_ref, bf16[2048,128]{1,0:T(8,128)(2,1)} %get-tuple-element.29.refs_1_, bf16[2,2048,128]{2,1,0:T(8,128)(2,1)} %get-tuple-element.31.refs_2_, bf16[2,2048,128]{2,1,0:T(8,128)(2,1)} %collective-permute-done.10.refs_3_), custom_call_target="tpu_custom_call" | custom-call | flops 8589934592 | bytes 2097152 | tf_op jit(solution)/shard_map/pallas_call | solution.py:253
  108.6 7.5 %spatial.1 = bf16[16,4,64,128]{3,2,1,0:T(8,128)(2,1)} custom-call(s32[8,8]{1,0:T(8,128)S(1)} %copy-done, bf16[16,3,4,64,128]{4,3,2,1,0:T(8,128)(2,1)S(1)} %all-to-all-done.1.qkv_ref), custom_call_target="tpu_custom_call" | custom-call | flops 4294967296 | bytes 4194304 | tf_op jit(solution)/shard_map/spatial/pallas_call | solution.py:338
  116.0 7.3 %all-to-all-start.2 = ((bf16[16,4,64,128]{3,2,1,0:T(8,128)(2,1)}), bf16[16,4,64,128]{3,2,1,0:T(8,128)(2,1)S(1)}, u32[]{:S(2)}, u32[]{:S(2)}) async-start(bf16[16,4,64,128]{3,2,1,0:T(8,128)(2,1)} %spatial.1), calls=%async_computation.2 | async-start | bytes 2097152 | tf_op jit(solution)/shard_map/all_to_all | solution.py:426
  123.4 13.7 %shard_map.56 = (f32[2048,128]{1,0:T(8,128)S(1)}, f32[2048,256]{1,0:T(8,128)S(1)}) custom-call(s32[1]{0:T(128)} %bitcast.refs_0_.strip_ref, bf16[2048,128]{1,0:T(8,128)(2,1)} %get-tuple-element.29.refs_1_, bf16[2,2048,128]{2,1,0:T(8,128)(2,1)} %collective-permute-done.7.refs_2_, bf16[2,2048,128]{2,1,0:T(8,128)(2,1)} %collective-permute-done.9.refs_3_, ...), custom_call_target="tpu_custom_call" | custom-call | flops 8589934592 | bytes 2097152 | tf_op jit(solution)/shard_map/pallas_call | solution.py:253
  137.1 7.5 %shard_map.57 = bf16[8,4,64,128]{3,2,1,0:T(8,128)(2,1)} custom-call(s32[1]{0:T(128)} %bitcast.refs_0_.strip_ref, bf16[2048,128]{1,0:T(8,128)(2,1)} %get-tuple-element.29.refs_1_, bf16[2,2048,128]{2,1,0:T(8,128)(2,1)} %collective-permute-done.8.refs_2_, f32[2048,128]{1,0:T(8,128)S(1)} %get-tuple-element.35.refs_3_, ...), custom_call_target="tpu_custom_call" | custom-call | flops 4294967296 | bytes 1048576 | tf_op jit(solution)/shard_map/pallas_call | solution.py:253
  144.6 5.2 %all-to-all-start = ((bf16[8,4,64,128]{3,2,1,0:T(8,128)(2,1)}), bf16[8,4,64,128]{3,2,1,0:T(8,128)(2,1)S(1)}, u32[]{:S(2)}, u32[]{:S(2)}) async-start(bf16[8,4,64,128]{3,2,1,0:T(8,128)(2,1)} %shard_map.57), calls=%async_computation | async-start | bytes 1048576 | tf_op jit(solution)/shard_map/all_to_all | solution.py:424
  149.8 1.1 join_spatial.1.refs_1_
  150.9 10.1 %all-to-all-done.refs_0_ = bf16[8,4,64,128]{3,2,1,0:T(8,128)(2,1)S(1)} async-done(((bf16[8,4,64,128]{3,2,1,0:T(8,128)(2,1)}), bf16[8,4,64,128]{3,2,1,0:T(8,128)(2,1)S(1)}, u32[]{:S(2)}, u32[]{:S(2)}) %all-to-all-start) | async-done | bytes 524320 | tf_op jit(solution)/shard_map/all_to_all | solution.py:424
  (16 shorter events, 1.7 us)
Async XLA Ops:
  4.0 104.5 %all-to-all-start.1 = ((bf16[16,3,4,64,128]{4,3,2,1,0:T(8,128)(2,1)}), bf16[16,3,4,64,128]{4,3,2,1,0:T(8,128)(2,1)S(1)}, u32[]{:S(2)}, u32[]{:S(2)}) async-start(bf16[16,3,4,64,128]{4,3,2,1,0:T(8,128)(2,1)} %split_spatial.1), calls=%async_computation.1 | async-start | bytes 6291456 | tf_op jit(solution)/shard_map/all_to_all | solution.py:398
  11.5 48.8 %collective-permute-start = (bf16[3,4,64,128]{3,2,1,0:T(8,128)(2,1)S(1)}, bf16[3,4,64,128]{3,2,1,0:T(8,128)(2,1)S(1)}, u32[]{:S(2)}, u32[]{:S(2)}) collective-permute-start(bf16[3,4,64,128]{3,2,1,0:T(8,128)(2,1)S(1)} %get-tuple-element.22), channel_id=1, source_target_pairs={{0,16},{16,0},{32,48},{48,32},{64,80},{80,64},{96,112},{112,96},{1... | collective-permute-start | bytes 589832 | tf_op jit(solution)/shard_map/ppermute | solution.py:385
  14.6 48.8 %collective-permute-start.1 = (bf16[3,4,64,128]{3,2,1,0:T(8,128)(2,1)S(1)}, bf16[3,4,64,128]{3,2,1,0:T(8,128)(2,1)S(1)}, u32[]{:S(2)}, u32[]{:S(2)}) collective-permute-start(bf16[3,4,64,128]{3,2,1,0:T(8,128)(2,1)S(1)} %get-tuple-element.23), channel_id=1, source_target_pairs={{0,32},{16,48},{32,0},{48,16},{64,96},{80,112},{96,64},{112,80},{1... | collective-permute-start | bytes 589832 | tf_op jit(solution)/shard_map/ppermute | solution.py:385
  16.1 47.4 %collective-permute-start.2 = (bf16[3,4,64,128]{3,2,1,0:T(8,128)(2,1)S(1)}, bf16[3,4,64,128]{3,2,1,0:T(8,128)(2,1)S(1)}, u32[]{:S(2)}, u32[]{:S(2)}) collective-permute-start(bf16[3,4,64,128]{3,2,1,0:T(8,128)(2,1)S(1)} %get-tuple-element.24), channel_id=1, source_target_pairs={{0,48},{16,32},{32,16},{48,0},{64,112},{80,96},{96,80},{112,64},{1... | collective-permute-start | bytes 589832 | tf_op jit(solution)/shard_map/ppermute | solution.py:385
  16.6 47.0 %collective-permute-start.3 = (bf16[3,4,64,128]{3,2,1,0:T(8,128)(2,1)S(1)}, bf16[3,4,64,128]{3,2,1,0:T(8,128)(2,1)S(1)}, u32[]{:S(2)}, u32[]{:S(2)}) collective-permute-start(bf16[3,4,64,128]{3,2,1,0:T(8,128)(2,1)S(1)} %get-tuple-element.25), channel_id=1, source_target_pairs={{0,64},{16,80},{32,96},{48,112},{64,0},{80,16},{96,32},{112,48},{1... | collective-permute-start | bytes 589832 | tf_op jit(solution)/shard_map/ppermute | solution.py:385
  19.8 43.8 %collective-permute-start.4 = (bf16[3,4,64,128]{3,2,1,0:T(8,128)(2,1)S(1)}, bf16[3,4,64,128]{3,2,1,0:T(8,128)(2,1)S(1)}, u32[]{:S(2)}, u32[]{:S(2)}) collective-permute-start(bf16[3,4,64,128]{3,2,1,0:T(8,128)(2,1)S(1)} %get-tuple-element.26), channel_id=1, source_target_pairs={{0,80},{16,64},{32,112},{48,96},{64,16},{80,0},{96,48},{112,32},{1... | collective-permute-start | bytes 589832 | tf_op jit(solution)/shard_map/ppermute | solution.py:385
  60.3 9.0 %collective-permute-start.5 = (bf16[3,4,64,128]{3,2,1,0:T(8,128)(2,1)S(1)}, bf16[3,4,64,128]{3,2,1,0:T(8,128)(2,1)S(1)}, u32[]{:S(2)}, u32[]{:S(2)}) collective-permute-start(bf16[3,4,64,128]{3,2,1,0:T(8,128)(2,1)S(1)} %get-tuple-element.27), channel_id=1, source_target_pairs={{0,96},{16,112},{32,64},{48,80},{64,32},{80,48},{96,0},{112,16},{1... | collective-permute-start | bytes 589832 | tf_op jit(solution)/shard_map/ppermute | solution.py:385
  63.3 9.7 %collective-permute-start.6 = (bf16[3,4,64,128]{3,2,1,0:T(8,128)(2,1)S(1)}, bf16[3,4,64,128]{3,2,1,0:T(8,128)(2,1)S(1)}, u32[]{:S(2)}, u32[]{:S(2)}) collective-permute-start(bf16[3,4,64,128]{3,2,1,0:T(8,128)(2,1)S(1)} %get-tuple-element.28), channel_id=1, source_target_pairs={{0,112},{16,96},{32,80},{48,64},{64,48},{80,32},{96,16},{112,0},{1... | collective-permute-start | bytes 589832 | tf_op jit(solution)/shard_map/ppermute | solution.py:385
  74.3 17.8 %collective-permute-start.7 = (bf16[2,2048,128]{2,1,0:T(8,128)(2,1)}, bf16[2,2048,128]{2,1,0:T(8,128)(2,1)}, u32[]{:S(2)}, u32[]{:S(2)}) collective-permute-start(bf16[2,2048,128]{2,1,0:T(8,128)(2,1)} %get-tuple-element.31.refs_2_), channel_id=1, source_target_pairs={{2,0},{4,2},{1,3},{6,4},{3,5},{8,6},{5,7},{10,8},{7,9},{12,10},{9,... | collective-permute-start | bytes 3145736 | tf_op jit(solution)/shard_map/ppermute | solution.py:406
  79.5 15.3 %collective-permute-start.10 = (bf16[2,2048,128]{2,1,0:T(8,128)(2,1)}, bf16[2,2048,128]{2,1,0:T(8,128)(2,1)}, u32[]{:S(2)}, u32[]{:S(2)}) collective-permute-start(bf16[2,2048,128]{2,1,0:T(8,128)(2,1)} %get-tuple-element.31.refs_2_), channel_id=1, source_target_pairs={{0,1},{1,0},{2,3},{3,2},{4,5},{5,4},{6,7},{7,6},{8,9},{9,8},{10,11... | collective-permute-start | bytes 3145736 | tf_op jit(solution)/shard_map/ppermute | solution.py:405
  92.1 45.0 %collective-permute-start.8 = (bf16[2,2048,128]{2,1,0:T(8,128)(2,1)}, bf16[2,2048,128]{2,1,0:T(8,128)(2,1)}, u32[]{:S(2)}, u32[]{:S(2)}) collective-permute-start(bf16[2,2048,128]{2,1,0:T(8,128)(2,1)} %get-tuple-element.31.refs_2_), channel_id=1, source_target_pairs={{3,1},{0,2},{5,3},{2,4},{7,5},{4,6},{9,7},{6,8},{11,9},{8,10},{13,... | collective-permute-start | bytes 3145736 | tf_op jit(solution)/shard_map/ppermute | solution.py:410
  94.6 28.7 %collective-permute-start.9 = (bf16[2,2048,128]{2,1,0:T(8,128)(2,1)}, bf16[2,2048,128]{2,1,0:T(8,128)(2,1)}, u32[]{:S(2)}, u32[]{:S(2)}) collective-permute-start(bf16[2,2048,128]{2,1,0:T(8,128)(2,1)} %collective-permute-done.7.refs_2_), channel_id=1, source_target_pairs={{0,1},{1,0},{2,3},{3,2},{4,5},{5,4},{6,7},{7,6},{8,9},{9,8},{10,11... | collective-permute-start | bytes 3145736 | tf_op jit(solution)/shard_map/ppermute | solution.py:413
  94.7 13.8 %copy-start = (s32[8,8]{1,0:T(8,128)S(1)}, s32[8,8]{1,0:T(8,128)}, u32[]{:S(2)}) copy-start(s32[8,8]{1,0:T(8,128)} %pick.1.mask_ref) | copy-start | bytes 772
  116.0 28.6 %all-to-all-start.2 = ((bf16[16,4,64,128]{3,2,1,0:T(8,128)(2,1)}), bf16[16,4,64,128]{3,2,1,0:T(8,128)(2,1)S(1)}, u32[]{:S(2)}, u32[]{:S(2)}) async-start(bf16[16,4,64,128]{3,2,1,0:T(8,128)(2,1)} %spatial.1), calls=%async_computation.2 | async-start | bytes 2097152 | tf_op jit(solution)/shard_map/all_to_all | solution.py:426
  144.6 16.3 %all-to-all-start = ((bf16[8,4,64,128]{3,2,1,0:T(8,128)(2,1)}), bf16[8,4,64,128]{3,2,1,0:T(8,128)(2,1)S(1)}, u32[]{:S(2)}, u32[]{:S(2)}) async-start(bf16[8,4,64,128]{3,2,1,0:T(8,128)(2,1)} %shard_map.57), calls=%async_computation | async-start | bytes 1048576 | tf_op jit(solution)/shard_map/all_to_all | solution.py:424
where the time goes:
time: 164 us; the launch traced here: 162 us
  waiting for transfers between devices  68.3 us (42%)
  Pallas kernels  52.9 us (32%)
  starting transfers between devices  40.5 us (25%)
    ppermute x7, waiting for transfers between devices, paired(): return lax.ppermute(block, 'frame', [(i, i ^ slot) for i in range(NF)])  47.3 us
    pallas_call x3, Pallas kernels, temporal(): pl.pallas_call(lambda *refs: temporal_kernel(offsets, state is not None,...  35 us
    ppermute x7, starting transfers between devices, paired(): return lax.ppermute(block, 'frame', [(i, i ^ slot) for i in range(NF)])  14.2 us
    ppermute x1, waiting for transfers between devices, main(): lax.ppermute(own, 'strip', [(s, i) for i, s in enumerate(shared_from) if...  10.9 us
    all_to_all x1, waiting for transfers between devices, main(): lax.all_to_all(t_out, 'frame', split_axis=0, concat_axis=0, tiled=True)  10.1 us
    pallas_call x1, Pallas kernels, spatial(): pl.pallas_call(spatial_kernel, in_specs=[scalars(), whole()], out_specs=a...  7.45 us
    all_to_all x1, starting transfers between devices, main(): lax.all_to_all(s_out, 'strip', split_axis=0, concat_axis=0, tiled=True)  7.34 us
    all_to_all x1, starting transfers between devices, main(): qkv = lax.all_to_all(qkv, 'strip', split_axis=0, concat_axis=0, tiled=True)  5.79 us
  transfers between devices with their start and end apart: 14, of which 5 were waited for; matrix products, arithmetic and copies ran while one was open for 0% of the time, Pallas kernels for 30%

commit v1 on v0

v1 whole, which is shorter than its diff:
```python
import functools
import math

import jax
import jax.numpy as jnp
from jax import lax
from jax.experimental import pallas as pl
from jax.experimental.pallas import tpu as pltpu
from jax.sharding import PartitionSpec as P


DH = 128
HS = 16
HT = 8
BLK = 128
NF = 8
NS = 16
QT = 512
QS = 256

NEG_FILL = -1e30
RATE = math.log2(math.e) / math.sqrt(DH)


BF16 = jnp.bfloat16
F32 = jnp.float32


def whole():
    return pl.BlockSpec(memory_space=pltpu.VMEM)


def scalars():
    return pl.BlockSpec(memory_space=pltpu.SMEM)


def anywhere():
    return pl.BlockSpec(memory_space=pl.ANY)


def in_vmem(block):
    return pltpu.with_memory_space_constraint(block, pltpu.VMEM)


def in_hbm(block):
    return pltpu.with_memory_space_constraint(block, pltpu.HBM)


def params(mib=8):
    return pltpu.CompilerParams(vmem_limit_bytes=mib * 1024 * 1024)


def load_parts(refs, frames, lanes, buf, sem):
    copies = [
        pltpu.make_async_copy(ref.at[frames, :, lanes], buf.at[part], sem.at[part])
        for part, ref in enumerate(refs)
    ]
    for copy in copies:
        copy.start()
    return copies


def split_spatial_kernel(first, q_ref, k_ref, v_ref, out_ref, buf, sem):
    frames = slice(first, first + out_ref.shape[2])
    copies = load_parts((q_ref, k_ref, v_ref), frames, slice(0, HS * DH), buf, sem)
    for part, copy in enumerate(copies):
        copy.wait()
        for head in range(HS):
            out_ref[head, part] = buf[part, :, :, head * DH : (head + 1) * DH]


def split_spatial(first, frames, queries, keys, values):
    spots = queries.shape[1]
    return pl.pallas_call(
        functools.partial(split_spatial_kernel, first),
        in_specs=[anywhere()] * 3,
        out_specs=whole(),
        out_shape=pltpu.HBM((HS, 3, frames, spots, DH), BF16),
        scratch_shapes=[
            pltpu.VMEM((3, frames, spots, HS * DH), BF16),
            pltpu.SemaphoreType.DMA((3,)),
        ],
        compiler_params=params(),
        name="split_spatial",
    )(in_hbm(queries), in_hbm(keys), in_hbm(values))


def split_temporal_kernel(group_ref, q_ref, k_ref, v_ref, *rest):
    out_refs, (buf, sem) = rest[:NF], rest[NF:]
    lanes = slice(HS * DH, (HS + HT) * DH)
    frames = slice(0, q_ref.shape[0])
    copies = load_parts((q_ref, k_ref, v_ref), frames, lanes, buf, sem)
    for part, copy in enumerate(copies):
        copy.wait()
        for slot in range(NF):
            at = pl.multiple_of(lax.bitwise_xor(group_ref[0], slot) * DH, DH)
            out_refs[slot][part] = buf[part, :, :, pl.ds(at, DH)]


def split_temporal(group, queries, keys, values):
    frames, spots, _ = queries.shape
    return pl.pallas_call(
        split_temporal_kernel,
        in_specs=[scalars()] + [anywhere()] * 3,
        out_specs=[whole()] * NF,
        out_shape=[pltpu.VMEM((3, frames, spots, DH), BF16)] * NF,
        scratch_shapes=[
            pltpu.VMEM((3, frames, spots, HT * DH), BF16),
            pltpu.SemaphoreType.DMA((3,)),
        ],
        compiler_params=params(),
        name="split_temporal",
    )(group, in_hbm(queries), in_hbm(keys), in_hbm(values))


def collect_kernel(*refs):
    slabs, q_ref, kv_ref = refs[:NF], refs[NF], refs[NF + 1]
    per = q_ref.shape[0] // NF
    for slot in range(NF):
        at = slice(slot * per, (slot + 1) * per)
        q_ref[at] = slabs[slot][0].reshape(per, DH)
        kv_ref[0, at] = slabs[slot][1].reshape(per, DH)
        kv_ref[1, at] = slabs[slot][2].reshape(per, DH)


def collect(slabs):
    _, frames, spots, _ = slabs[0].shape
    rows = NF * frames * spots
    return pl.pallas_call(
        collect_kernel,
        in_specs=[whole()] * NF,
        out_specs=[whole()] * 2,
        out_shape=[pltpu.HBM((rows, DH), BF16), pltpu.VMEM((2, rows, DH), BF16)],
        compiler_params=params(),
        name="collect",
    )(*[in_vmem(slab) for slab in slabs])


def scores_of(q, k):
    return lax.dot_general(q, k, (((1,), (1,)), ((), ())), preferred_element_type=F32)


def with_ones(v):
    return jnp.concatenate([v, jnp.ones_like(v)], axis=1)


def usable(strip_ref, offset):
    source = strip_ref[0] + offset * (1 - 2 * lax.rem(strip_ref[0], 2))
    return (source >= 0) & (source < NS)


def attend(q_ref, kv_ref, s_buf, state, done):
    k = kv_ref[0]
    tiles = q_ref.shape[0] // QT

    def raw(i):
        return scores_of(q_ref[i * QT : (i + 1) * QT], k)

    s_buf[0] = raw(0)
    for i in range(tiles):
        if i + 1 < tiles:
            s_buf[(i + 1) % 2] = raw(i + 1)
        at = slice(i * QT, (i + 1) * QT)
        s = s_buf[i % 2]
        top = jnp.broadcast_to(jnp.max(s, axis=1, keepdims=True), (QT, DH))
        if state is not None:
            before = state[0][at]
            top = jnp.maximum(before, top)
            fade = jnp.exp2((before - top) * RATE)
        weights = jnp.exp2((s - top[:, :1]) * RATE).astype(BF16)
        mixed = jnp.dot(weights, with_ones(kv_ref[1]), preferred_element_type=F32)
        if state is not None:
            mixed = mixed + state[1][at] * jnp.concatenate([fade, fade], axis=1)
        done(i, top, mixed)


def temporal_kernel(offsets, resume, strip_ref, q_ref, *refs):
    count = len(offsets)
    kv_refs, rest = refs[:count], refs[count:]
    if resume:
        old_top, old_mix, top_ref, mix_ref, s_buf, sem = rest
        loads = [
            pltpu.make_async_copy(old_top, top_ref, sem.at[0]),
            pltpu.make_async_copy(old_mix, mix_ref, sem.at[1]),
        ]
        for load in loads:
            load.start()
        for load in loads:
            load.wait()
    else:
        top_ref, mix_ref, s_buf = rest

    def done(i, top, mixed):
        at = slice(i * QT, (i + 1) * QT)
        top_ref[at] = top
        mix_ref[at] = mixed

    for offset, kv_ref in zip(offsets, kv_refs):
        if offset == 0:
            attend(q_ref, kv_ref, s_buf, None, done)
        else:
            pl.when(usable(strip_ref, offset))(
                lambda kv_ref=kv_ref: attend(q_ref, kv_ref, s_buf, (top_ref, mix_ref), done)
            )


def temporal(strip, q, strips, state=None):
    rows = q.shape[0]
    count = len(strips)
    state_shape = [((rows, DH), F32), ((rows, 2 * DH), F32)]
    args = [strip, in_hbm(q), *[in_vmem(x) for x in strips.values()]]
    in_specs = [scalars()] + [whole()] * (1 + count)
    scratch = [pltpu.VMEM((2, QT, rows), F32)]
    if state is not None:
        args += [in_hbm(x) for x in state]
        in_specs += [anywhere()] * 2
        scratch.append(pltpu.SemaphoreType.DMA((2,)))
    space = pltpu.HBM if state is None else pltpu.VMEM
    cost = pl.CostEstimate(
        flops=count * rows**2 * DH * 8,
        transcendentals=count * rows**2,
        bytes_accessed=count * rows * DH * 4,
    )
    return pl.pallas_call(
        functools.partial(temporal_kernel, tuple(strips), state is not None),
        in_specs=in_specs,
        out_specs=[whole()] * 2,
        out_shape=[space(*shape) for shape in state_shape],
        scratch_shapes=scratch,
        compiler_params=params(20),
        cost_estimate=cost,
    )(*args)


def temporal_last_kernel(offset, strip_ref, group_ref, q_ref, kv_ref, top_ref, mix_ref, *rest):
    out_ref, s_buf = rest
    per = q_ref.shape[0] // NF
    slots = QT // per

    def done(i, _, mixed):
        for r in range(slots):
            rows = mixed[r * per : (r + 1) * per]
            result = (rows[:, :DH] / rows[:, DH:]).astype(BF16)
            target = lax.bitwise_xor(group_ref[0], i * slots + r)
            out_ref[target] = result.reshape(out_ref.shape[1:])

    valid = usable(strip_ref, offset)
    pl.when(valid)(lambda: attend(q_ref, kv_ref, s_buf, (top_ref, mix_ref), done))

    @pl.when(jnp.logical_not(valid))
    def _():
        for i in range(NF // slots):
            done(i, None, mix_ref[i * QT : (i + 1) * QT])


def temporal_last(strip, group, q, offset, kv, state, shape):
    rows = q.shape[0]
    return pl.pallas_call(
        functools.partial(temporal_last_kernel, offset),
        in_specs=[scalars()] * 2 + [whole()] * 4,
        out_specs=whole(),
        out_shape=pltpu.HBM(shape, BF16),
        scratch_shapes=[pltpu.VMEM((2, QT, rows), F32)],
        compiler_params=params(20),
        cost_estimate=pl.CostEstimate(
            flops=rows**2 * DH * 8, transcendentals=rows**2, bytes_accessed=rows * DH * 4
        ),
        name="temporal_last",
    )(strip, group, in_hbm(q), *[in_vmem(x) for x in (kv, *state)])


def spatial_kernel(first, strip_ref, pattern_ref, mask_ref, qkv_ref, *rest):
    pattern = pattern_ref[strip_ref[0]]
    out_ref, s_buf, result_ref, sem = rest[-4:]
    frames, strips, spots, _ = result_ref.shape
    positions = strips * spots
    blocks = positions // BLK
    tiles = positions // QS
    per = QS // spots

    def raw(f, i):
        q = qkv_ref[i * per : (i + 1) * per, 0, f].reshape(QS, DH)
        return scores_of(q, qkv_ref[:, 1, f].reshape(positions, DH))

    def masked(s, i):
        rows = []
        for r in range(QS // BLK):
            row = i * (QS // BLK) + r
            cells = []
            for j in range(blocks):
                bias = jnp.where(mask_ref[pattern, row, j] > 0, 0.0, NEG_FILL)
                cells.append(s[r * BLK : (r + 1) * BLK, j * BLK : (j + 1) * BLK] + bias)
            rows.append(jnp.concatenate(cells, axis=1))
        return jnp.concatenate(rows, axis=0)

    s_buf[0] = raw(0, 0)

    def frame(f, carry):
        v = with_ones(qkv_ref[:, 2, f].reshape(positions, DH))
        for i in range(tiles):
            if i + 1 < tiles:
                s_buf[(i + 1) % 2] = raw(f, i + 1)
            else:
                s_buf[(i + 1) % 2] = raw(jnp.minimum(f + 1, frames - 1), 0)
            s = masked(s_buf[i % 2], i)
            top = jnp.max(s, axis=1, keepdims=True)
            weights = jnp.exp2((s - top) * RATE).astype(BF16)
            mixed = jnp.dot(weights, v, preferred_element_type=F32)
            result = (mixed[:, :DH] / mixed[:, DH:]).astype(BF16)
            result_ref[f, i * per : (i + 1) * per] = result.reshape(per, spots, DH)
        leave(f).start()
        return carry

    def leave(f):
        return pltpu.make_async_copy(result_ref.at[f], out_ref.at[:, first + f], sem.at[f])

    lax.fori_loop(0, frames, frame, 0)
    for f in range(frames):
        leave(f).wait()


def spatial(first, frames_all, strip, head_pattern, masks, qkv, partial=None):
    strips, _, frames, spots, _ = qkv.shape
    positions = strips * spots
    cost = pl.CostEstimate(
        flops=frames * positions**2 * DH * 8,
        transcendentals=frames * positions**2,
        bytes_accessed=4 * strips * frames * spots * DH * 2,
    )
    args = [strip, head_pattern, masks, in_vmem(qkv)]
    if partial is not None:
        args.append(in_hbm(partial))
    return pl.pallas_call(
        functools.partial(spatial_kernel, first),
        in_specs=[*[scalars()] * 3, whole(), anywhere()][: len(args)],
        out_specs=anywhere(),
        scratch_shapes=[
            pltpu.VMEM((2, QS, positions), F32),
            pltpu.VMEM((frames, strips, spots, DH), BF16),
            pltpu.SemaphoreType.DMA((frames,)),
        ],
        out_shape=pltpu.HBM((strips, frames_all, spots, DH), BF16),
        input_output_aliases={} if partial is None else {4: 0},
        compiler_params=params(12),
        cost_estimate=cost,
        name="spatial",
    )(*args)


def join_kernel(first, heads_ref, *rest):
    out_ref, sem = rest[-2:]
    copies = []
    for head in range(heads_ref.shape[0]):
        at = (first + head) * DH
        copies.append(
            pltpu.make_async_copy(heads_ref.at[head], out_ref.at[:, :, at : at + DH], sem.at[head])
        )
        copies[-1].start()
    for copy in copies:
        copy.wait()


def join(heads, first, partial=None):
    count, frames, spots, _ = heads.shape
    args = [in_vmem(heads)]
    if partial is not None:
        args.append(partial)
    return pl.pallas_call(
        lambda *refs: join_kernel(first, *refs),
        in_specs=[whole(), anywhere()][: len(args)],
        out_specs=anywhere(),
        out_shape=jax.ShapeDtypeStruct((frames, spots, (HS + HT) * DH), BF16),
        scratch_shapes=[pltpu.SemaphoreType.DMA((count,))],
        input_output_aliases={} if partial is None else {1: 0},
        compiler_params=params(),
        name="join_spatial" if partial is None else "join_temporal",
    )(*args)


def paired(block, slot):
    return lax.ppermute(block, "frame", [(i, i ^ slot) for i in range(NF)])


def main(queries, keys, values, block_masks, head_pattern):
    frames, spots, _ = queries.shape
    group = lax.axis_index("frame").astype(jnp.int32)
    strip = lax.axis_index("strip").astype(jnp.int32)
    group_arg = group.reshape(1)
    strip_arg = strip.reshape(1)

    half = frames // 2
    qkv_a = split_spatial(0, half, queries, keys, values)
    qkv_a = lax.all_to_all(qkv_a, "strip", split_axis=0, concat_axis=0, tiled=True)
    slabs = split_temporal(group_arg, queries, keys, values)
    slabs = [slabs[0]] + [paired(slabs[d], d) for d in range(1, NF)]
    qkv_b = split_spatial(half, half, queries, keys, values)
    qkv_b = lax.all_to_all(qkv_b, "strip", split_axis=0, concat_axis=0, tiled=True)
    t_q, own = collect(slabs)

    swap = [(i, i ^ 1) for i in range(NS)]
    shared_from = [i + 2 if i % 2 == 0 else i - 2 for i in range(NS)]
    single_from = [i - 2 if i % 2 == 0 else i + 2 for i in range(NS)]
    partner = lax.ppermute(own, "strip", swap)
    shared = lax.ppermute(own, "strip", [(s, i) for i, s in enumerate(shared_from) if 0 <= s < NS])
    own_later, shared = lax.optimization_barrier((own, shared))
    single = lax.ppermute(
        own_later, "strip", [(s, i) for i, s in enumerate(single_from) if 0 <= s < NS]
    )
    passed = lax.ppermute(shared, "strip", swap)

    state = temporal(strip_arg, t_q, {0: own, 1: partner})
    state = temporal(strip_arg, t_q, {2: shared, -1: passed}, state)
    t_out = temporal_last(
        strip_arg, group_arg, t_q, -2, single, state, (NF, frames, spots, DH)
    )
    t_out = lax.all_to_all(t_out, "frame", split_axis=0, concat_axis=0, tiled=True)
    s_out = spatial(0, frames, strip_arg, head_pattern, block_masks, qkv_a)
    s_out = spatial(half, frames, strip_arg, head_pattern, block_masks, qkv_b, s_out)
    s_out = lax.all_to_all(s_out, "strip", split_axis=0, concat_axis=0, tiled=True)
    partial = join(s_out, 0)
    return join(t_out, HS, partial)


def solution(mesh):
    spec = P("frame", "strip", None)
    return jax.shard_map(
        main,
        mesh=mesh,
        in_specs=(spec, spec, spec, P(), P()),
        out_specs=spec,
        check_vma=False,
    )
```

time: 164 us -> 161 us (0.982)
  waiting for transfers between devices: 68.3 us -> 59.5 us
  starting transfers between devices: 40.5 us -> 44.5 us
  Pallas kernels: 52.9 us -> 54.7 us
    ppermute x7, waiting for transfers between devices: 47.3 us -> 30.6 us  [paired(): return lax.ppermute(block, 'frame', [(i, i ^ slot) for i in range(NF)])]
    ppermute x1, waiting for transfers between devices: 10.9 us -> 18.8 us  [main(): lax.ppermute(own, 'strip', [(s, i) for i, s in enumerate(shared_from) if...]
    all_to_all x1 -> x2, starting transfers between devices: 5.79 us -> 9.89 us  [the longest x1 5.79 us: main(): lax.all_to_all(qkv_a, 'strip', split_axis=0, concat_axis=0, tiled=True)]
    pallas_call x6 -> x7, Pallas kernels: 48.1 us -> 50 us  [the longest x2 27.6 us: temporal(): pl.pallas_call(functools.partial(temporal_kernel, tuple(strips), state is...]
  transfers between devices with their start and end apart: 14 -> 15, of which waited for: 5 -> 5; matrix products, arithmetic and copies ran while one was open for 0% -> 0% of each run, Pallas kernels for 30% -> 32%
where the time goes in v1:
time: 161 us; the launch traced here: 159 us
  waiting for transfers between devices  59.5 us (37%)
  Pallas kernels  54.7 us (34%)
  starting transfers between devices  44.5 us (28%)
    ppermute x7, waiting for transfers between devices, paired(): return lax.ppermute(block, 'frame', [(i, i ^ slot) for i in range(NF)])  30.6 us
    pallas_call x2, Pallas kernels, temporal(): pl.pallas_call(functools.partial(temporal_kernel, tuple(strips), state is...  27.6 us
    ppermute x1, waiting for transfers between devices, main(): lax.ppermute(own, 'strip', [(s, i) for i, s in enumerate(shared_from) if...  18.8 us
    ppermute x7, starting transfers between devices, paired(): return lax.ppermute(block, 'frame', [(i, i ^ slot) for i in range(NF)])  14.2 us
    all_to_all x1, waiting for transfers between devices, main(): lax.all_to_all(t_out, 'frame', split_axis=0, concat_axis=0, tiled=True)  10.1 us
    pallas_call x2, Pallas kernels, spatial(): pl.pallas_call(functools.partial(spatial_kernel, first), in_specs=[*[scal...  9.57 us
    all_to_all x1, starting transfers between devices, main(): lax.all_to_all(s_out, 'strip', split_axis=0, concat_axis=0, tiled=True)  8.33 us
    pallas_call x1, Pallas kernels, temporal_last(): pl.pallas_call(functools.partial(temporal_last_kernel, offset), in_specs=...  7.53 us
  transfers between devices with their start and end apart: 15, of which 5 were waited for; matrix products, arithmetic and copies ran while one was open for 0% of the time, Pallas kernels for 32%

profile of v1, /device:TPU:32, one launch (start us, length us, event | category | flops | bytes accessed | tf_op | source)
XLA Modules:
  0.0 159.0 jit_solution(7584875746800754588)
XLA Ops:
  0.0 2.6 %split_spatial.3 = bf16[16,3,2,64,128]{4,3,2,1,0:T(8,128)(2,1)} custom-call(bf16[4,64,3072]{2,1,0:T(8,128)(2,1)} %q_ref.5, bf16[4,64,3072]{2,1,0:T(8,128)(2,1)} %k_ref.5, bf16[4,64,3072]{2,1,0:T(8,128)(2,1)} %v_ref.5), custom_call_target="tpu_custom_call" | custom-call | tf_op jit(solution)/shard_map/split_spatial/pallas_call | solution.py:74
  2.6 5.8 %all-to-all-start.2 = ((bf16[16,3,2,64,128]{4,3,2,1,0:T(8,128)(2,1)}), bf16[16,3,2,64,128]{4,3,2,1,0:T(8,128)(2,1)S(1)}, u32[]{:S(2)}, u32[]{:S(2)}) async-start(bf16[16,3,2,64,128]{4,3,2,1,0:T(8,128)(2,1)} %split_spatial.3), calls=%async_computation.2 | async-start | bytes 3145728 | tf_op jit(solution)/shard_map/all_to_all | solution.py:393
  8.4 1.5 split_temporal.1
  10.0 3.1 %collective-permute-start = (bf16[3,4,64,128]{3,2,1,0:T(8,128)(2,1)S(1)}, bf16[3,4,64,128]{3,2,1,0:T(8,128)(2,1)S(1)}, u32[]{:S(2)}, u32[]{:S(2)}) collective-permute-start(bf16[3,4,64,128]{3,2,1,0:T(8,128)(2,1)S(1)} %get-tuple-element.22), channel_id=1, source_target_pairs={{0,16},{16,0},{32,48},{48,32},{64,80},{80,64},{96,112},{112,96},{1... | collective-permute-start | bytes 589832 | tf_op jit(solution)/shard_map/ppermute | solution.py:381
  13.0 1.6 collective-permute-start.1
  15.0 3.2 %collective-permute-start.3 = (bf16[3,4,64,128]{3,2,1,0:T(8,128)(2,1)S(1)}, bf16[3,4,64,128]{3,2,1,0:T(8,128)(2,1)S(1)}, u32[]{:S(2)}, u32[]{:S(2)}) collective-permute-start(bf16[3,4,64,128]{3,2,1,0:T(8,128)(2,1)S(1)} %get-tuple-element.25), channel_id=1, source_target_pairs={{0,64},{16,80},{32,96},{48,112},{64,0},{80,16},{96,32},{112,48},{1... | collective-permute-start | bytes 589832 | tf_op jit(solution)/shard_map/ppermute | solution.py:381
  18.2 2.7 %collective-permute-start.4 = (bf16[3,4,64,128]{3,2,1,0:T(8,128)(2,1)S(1)}, bf16[3,4,64,128]{3,2,1,0:T(8,128)(2,1)S(1)}, u32[]{:S(2)}, u32[]{:S(2)}) collective-permute-start(bf16[3,4,64,128]{3,2,1,0:T(8,128)(2,1)S(1)} %get-tuple-element.26), channel_id=1, source_target_pairs={{0,80},{16,64},{32,112},{48,96},{64,16},{80,0},{96,48},{112,32},{1... | collective-permute-start | bytes 589832 | tf_op jit(solution)/shard_map/ppermute | solution.py:381
  21.0 21.1 %collective-permute-done.refs_1_ = bf16[3,4,64,128]{3,2,1,0:T(8,128)(2,1)S(1)} collective-permute-done((bf16[3,4,64,128]{3,2,1,0:T(8,128)(2,1)S(1)}, bf16[3,4,64,128]{3,2,1,0:T(8,128)(2,1)S(1)}, u32[]{:S(2)}, u32[]{:S(2)}) %collective-permute-start) | collective-permute-done | bytes 196640 | tf_op jit(solution)/shard_map/ppermute | solution.py:381
  42.1 3.0 %collective-permute-start.5 = (bf16[3,4,64,128]{3,2,1,0:T(8,128)(2,1)S(1)}, bf16[3,4,64,128]{3,2,1,0:T(8,128)(2,1)S(1)}, u32[]{:S(2)}, u32[]{:S(2)}) collective-permute-start(bf16[3,4,64,128]{3,2,1,0:T(8,128)(2,1)S(1)} %get-tuple-element.27), channel_id=1, source_target_pairs={{0,96},{16,112},{32,64},{48,80},{64,32},{80,48},{96,0},{112,16},{1... | collective-permute-start | bytes 589832 | tf_op jit(solution)/shard_map/ppermute | solution.py:381
  45.3 5.7 %collective-permute-done.5.refs_6_ = bf16[3,4,64,128]{3,2,1,0:T(8,128)(2,1)S(1)} collective-permute-done((bf16[3,4,64,128]{3,2,1,0:T(8,128)(2,1)S(1)}, bf16[3,4,64,128]{3,2,1,0:T(8,128)(2,1)S(1)}, u32[]{:S(2)}, u32[]{:S(2)}) %collective-permute-start.5) | collective-permute-done | bytes 196640 | tf_op jit(solution)/shard_map/ppermute | solution.py:381
  51.0 3.7 %collective-permute-done.6.refs_7_ = bf16[3,4,64,128]{3,2,1,0:T(8,128)(2,1)S(1)} collective-permute-done((bf16[3,4,64,128]{3,2,1,0:T(8,128)(2,1)S(1)}, bf16[3,4,64,128]{3,2,1,0:T(8,128)(2,1)S(1)}, u32[]{:S(2)}, u32[]{:S(2)}) %collective-permute-start.6) | collective-permute-done | bytes 196640 | tf_op jit(solution)/shard_map/ppermute | solution.py:381
  56.0 5.2 %collective-permute-start.7 = (bf16[2,2048,128]{2,1,0:T(8,128)(2,1)}, bf16[2,2048,128]{2,1,0:T(8,128)(2,1)}, u32[]{:S(2)}, u32[]{:S(2)}) collective-permute-start(bf16[2,2048,128]{2,1,0:T(8,128)(2,1)} %get-tuple-element.31.refs_0_), channel_id=1, source_target_pairs={{2,0},{4,2},{1,3},{6,4},{3,5},{8,6},{5,7},{10,8},{7,9},{12,10},{9,... | collective-permute-start | bytes 3145736 | tf_op jit(solution)/shard_map/ppermute | solution.py:404
  61.3 2.6 %split_spatial.2 = bf16[16,3,2,64,128]{4,3,2,1,0:T(8,128)(2,1)} custom-call(bf16[4,64,3072]{2,1,0:T(8,128)(2,1)} %q_ref.5, bf16[4,64,3072]{2,1,0:T(8,128)(2,1)} %k_ref.5, bf16[4,64,3072]{2,1,0:T(8,128)(2,1)} %v_ref.5), custom_call_target="tpu_custom_call" | custom-call | tf_op jit(solution)/shard_map/split_spatial/pallas_call | solution.py:74
  63.9 4.1 %all-to-all-start.1 = ((bf16[16,3,2,64,128]{4,3,2,1,0:T(8,128)(2,1)}), bf16[16,3,2,64,128]{4,3,2,1,0:T(8,128)(2,1)S(1)}, u32[]{:S(2)}, u32[]{:S(2)}) async-start(bf16[16,3,2,64,128]{4,3,2,1,0:T(8,128)(2,1)} %split_spatial.2), calls=%async_computation.1 | async-start | bytes 3145728 | tf_op jit(solution)/shard_map/all_to_all | solution.py:397
  68.0 18.8 %collective-permute-done.7.refs_0_ = bf16[2,2048,128]{2,1,0:T(8,128)(2,1)} collective-permute-done((bf16[2,2048,128]{2,1,0:T(8,128)(2,1)}, bf16[2,2048,128]{2,1,0:T(8,128)(2,1)}, u32[]{:S(2)}, u32[]{:S(2)}) %collective-permute-start.7) | collective-permute-done | bytes 1048608 | tf_op jit(solution)/shard_map/ppermute | solution.py:404
  86.9 1.9 %collective-permute-start.8 = (bf16[2,2048,128]{2,1,0:T(8,128)(2,1)}, bf16[2,2048,128]{2,1,0:T(8,128)(2,1)}, u32[]{:S(2)}, u32[]{:S(2)}) collective-permute-start(bf16[2,2048,128]{2,1,0:T(8,128)(2,1)} %get-tuple-element.31.refs_0_), channel_id=1, source_target_pairs={{3,1},{0,2},{5,3},{2,4},{7,5},{4,6},{9,7},{6,8},{11,9},{8,10},{13,... | collective-permute-start | bytes 3145736 | tf_op jit(solution)/shard_map/ppermute | solution.py:406
  88.9 13.8 %shard_map.55 = (f32[2048,128]{1,0:T(8,128)}, f32[2048,256]{1,0:T(8,128)}) custom-call(s32[1]{0:T(128)} %bitcast.strip_ref, bf16[2048,128]{1,0:T(8,128)(2,1)} %get-tuple-element.29.q_ref, bf16[2,2048,128]{2,1,0:T(8,128)(2,1)} %get-tuple-element.31.refs_0_, bf16[2,2048,128]{2,1,0:T(8,128)(2,1)} %collective-permute-done.10.refs_1_), custom_call_target="tpu_custom_call" | custom-call | flops 8589934592 | bytes 2097152 | tf_op jit(solution)/shard_map/pallas_call | solution.py:224
  102.8 4.8 %spatial.2.rest_0_ = bf16[16,4,64,128]{3,2,1,0:T(8,128)(2,1)} custom-call(s32[1]{0:T(128)} %bitcast.strip_ref, s32[16]{0:T(128)S(1)} %copy-done.1, s32[4,8,8]{2,1,0:T(8,128)S(1)} %copy-done, bf16[16,3,2,64,128]{4,3,2,1,0:T(8,128)(2,1)S(1)} %all-to-all-done.2.qkv_ref), custom_call_target="tpu_custom_call" | custom-call | flops 2147483648 | bytes 2097152 | tf_op jit(solution)/shard_map/spatial/pallas_call | solution.py:333
  107.6 4.8 %spatial.3 = bf16[16,4,64,128]{3,2,1,0:T(8,128)(2,1)} custom-call(s32[1]{0:T(128)} %bitcast.strip_ref, s32[16]{0:T(128)S(1)} %copy-done.1, s32[4,8,8]{2,1,0:T(8,128)S(1)} %copy-done, bf16[16,3,2,64,128]{4,3,2,1,0:T(8,128)(2,1)S(1)} %all-to-all-done.1.qkv_ref, bf16[16,4,64,128]{3,2,1,0:T(8,128)(2,1)} %spatial.2.rest_0_), custom_call_target="tpu_custom_call", output_to_operand_aliasing={{}: (4, {})} | custom-call | flops 2147483648 | bytes 2097152 | tf_op jit(solution)/shard_map/spatial/pallas_call | solution.py:333
  112.4 8.3 %all-to-all-start.3 = ((bf16[16,4,64,128]{3,2,1,0:T(8,128)(2,1)}), bf16[16,4,64,128]{3,2,1,0:T(8,128)(2,1)S(1)}, u32[]{:S(2)}, u32[]{:S(2)}) async-start(bf16[16,4,64,128]{3,2,1,0:T(8,128)(2,1)} %spatial.3), calls=%async_computation.3 | async-start | bytes 2097152 | tf_op jit(solution)/shard_map/all_to_all | solution.py:419
  120.7 13.8 %shard_map.56 = (f32[2048,128]{1,0:T(8,128)S(1)}, f32[2048,256]{1,0:T(8,128)S(1)}) custom-call(s32[1]{0:T(128)} %bitcast.strip_ref, bf16[2048,128]{1,0:T(8,128)(2,1)} %get-tuple-element.29.q_ref, bf16[2,2048,128]{2,1,0:T(8,128)(2,1)} %collective-permute-done.7.refs_0_, bf16[2,2048,128]{2,1,0:T(8,128)(2,1)} %collective-permute-done.9.refs_1_, ...), custom_call_target="tpu_custom_call" | custom-call | flops 8589934592 | bytes 2097152 | tf_op jit(solution)/shard_map/pallas_call | solution.py:224
  134.5 7.5 %temporal_last.1 = bf16[8,4,64,128]{3,2,1,0:T(8,128)(2,1)} custom-call(s32[1]{0:T(128)} %bitcast.strip_ref, s32[1]{0:T(128)} %bitcast.1.group_ref, bf16[2048,128]{1,0:T(8,128)(2,1)} %get-tuple-element.29.q_ref, bf16[2,2048,128]{2,1,0:T(8,128)(2,1)} %collective-permute-done.8.kv_ref, f32[2048,128]{1,0:T(8,128)S(1)} %get-tuple-element.35.top_ref, ...), custom_call_target="tpu_custom_call" | custom-call | flops 4294967296 | bytes 1048576 | tf_op jit(solution)/shard_map/temporal_last/pallas_call | solution.py:258
  142.0 4.8 %all-to-all-start = ((bf16[8,4,64,128]{3,2,1,0:T(8,128)(2,1)}), bf16[8,4,64,128]{3,2,1,0:T(8,128)(2,1)S(1)}, u32[]{:S(2)}, u32[]{:S(2)}) async-start(bf16[8,4,64,128]{3,2,1,0:T(8,128)(2,1)} %temporal_last.1), calls=%async_computation | async-start | bytes 1048576 | tf_op jit(solution)/shard_map/all_to_all | solution.py:416
  147.9 10.1 %all-to-all-done.refs_0_ = bf16[8,4,64,128]{3,2,1,0:T(8,128)(2,1)S(1)} async-done(((bf16[8,4,64,128]{3,2,1,0:T(8,128)(2,1)}), bf16[8,4,64,128]{3,2,1,0:T(8,128)(2,1)S(1)}, u32[]{:S(2)}, u32[]{:S(2)}) %all-to-all-start) | async-done | bytes 524320 | tf_op jit(solution)/shard_map/all_to_all | solution.py:416
  (21 shorter events, 4.1 us)
Async XLA Ops:
  2.6 61.3 %all-to-all-start.2 = ((bf16[16,3,2,64,128]{4,3,2,1,0:T(8,128)(2,1)}), bf16[16,3,2,64,128]{4,3,2,1,0:T(8,128)(2,1)S(1)}, u32[]{:S(2)}, u32[]{:S(2)}) async-start(bf16[16,3,2,64,128]{4,3,2,1,0:T(8,128)(2,1)} %split_spatial.3), calls=%async_computation.2 | async-start | bytes 3145728 | tf_op jit(solution)/shard_map/all_to_all | solution.py:393
  10.0 32.1 %collective-permute-start = (bf16[3,4,64,128]{3,2,1,0:T(8,128)(2,1)S(1)}, bf16[3,4,64,128]{3,2,1,0:T(8,128)(2,1)S(1)}, u32[]{:S(2)}, u32[]{:S(2)}) collective-permute-start(bf16[3,4,64,128]{3,2,1,0:T(8,128)(2,1)S(1)} %get-tuple-element.22), channel_id=1, source_target_pairs={{0,16},{16,0},{32,48},{48,32},{64,80},{80,64},{96,112},{112,96},{1... | collective-permute-start | bytes 589832 | tf_op jit(solution)/shard_map/ppermute | solution.py:381
  13.0 32.1 %collective-permute-start.1 = (bf16[3,4,64,128]{3,2,1,0:T(8,128)(2,1)S(1)}, bf16[3,4,64,128]{3,2,1,0:T(8,128)(2,1)S(1)}, u32[]{:S(2)}, u32[]{:S(2)}) collective-permute-start(bf16[3,4,64,128]{3,2,1,0:T(8,128)(2,1)S(1)} %get-tuple-element.23), channel_id=1, source_target_pairs={{0,32},{16,48},{32,0},{48,16},{64,96},{80,112},{96,64},{112,80},{1... | collective-permute-start | bytes 589832 | tf_op jit(solution)/shard_map/ppermute | solution.py:381
  14.6 30.7 %collective-permute-start.2 = (bf16[3,4,64,128]{3,2,1,0:T(8,128)(2,1)S(1)}, bf16[3,4,64,128]{3,2,1,0:T(8,128)(2,1)S(1)}, u32[]{:S(2)}, u32[]{:S(2)}) collective-permute-start(bf16[3,4,64,128]{3,2,1,0:T(8,128)(2,1)S(1)} %get-tuple-element.24), channel_id=1, source_target_pairs={{0,48},{16,32},{32,16},{48,0},{64,112},{80,96},{96,80},{112,64},{1... | collective-permute-start | bytes 589832 | tf_op jit(solution)/shard_map/ppermute | solution.py:381
  15.0 30.3 %collective-permute-start.3 = (bf16[3,4,64,128]{3,2,1,0:T(8,128)(2,1)S(1)}, bf16[3,4,64,128]{3,2,1,0:T(8,128)(2,1)S(1)}, u32[]{:S(2)}, u32[]{:S(2)}) collective-permute-start(bf16[3,4,64,128]{3,2,1,0:T(8,128)(2,1)S(1)} %get-tuple-element.25), channel_id=1, source_target_pairs={{0,64},{16,80},{32,96},{48,112},{64,0},{80,16},{96,32},{112,48},{1... | collective-permute-start | bytes 589832 | tf_op jit(solution)/shard_map/ppermute | solution.py:381
  18.2 27.1 %collective-permute-start.4 = (bf16[3,4,64,128]{3,2,1,0:T(8,128)(2,1)S(1)}, bf16[3,4,64,128]{3,2,1,0:T(8,128)(2,1)S(1)}, u32[]{:S(2)}, u32[]{:S(2)}) collective-permute-start(bf16[3,4,64,128]{3,2,1,0:T(8,128)(2,1)S(1)} %get-tuple-element.26), channel_id=1, source_target_pairs={{0,80},{16,64},{32,112},{48,96},{64,16},{80,0},{96,48},{112,32},{1... | collective-permute-start | bytes 589832 | tf_op jit(solution)/shard_map/ppermute | solution.py:381
  42.1 9.0 %collective-permute-start.5 = (bf16[3,4,64,128]{3,2,1,0:T(8,128)(2,1)S(1)}, bf16[3,4,64,128]{3,2,1,0:T(8,128)(2,1)S(1)}, u32[]{:S(2)}, u32[]{:S(2)}) collective-permute-start(bf16[3,4,64,128]{3,2,1,0:T(8,128)(2,1)S(1)} %get-tuple-element.27), channel_id=1, source_target_pairs={{0,96},{16,112},{32,64},{48,80},{64,32},{80,48},{96,0},{112,16},{1... | collective-permute-start | bytes 589832 | tf_op jit(solution)/shard_map/ppermute | solution.py:381
  45.1 9.7 %collective-permute-start.6 = (bf16[3,4,64,128]{3,2,1,0:T(8,128)(2,1)S(1)}, bf16[3,4,64,128]{3,2,1,0:T(8,128)(2,1)S(1)}, u32[]{:S(2)}, u32[]{:S(2)}) collective-permute-start(bf16[3,4,64,128]{3,2,1,0:T(8,128)(2,1)S(1)} %get-tuple-element.28), channel_id=1, source_target_pairs={{0,112},{16,96},{32,80},{48,64},{64,48},{80,32},{96,16},{112,0},{1... | collective-permute-start | bytes 589832 | tf_op jit(solution)/shard_map/ppermute | solution.py:381
  56.0 30.8 %collective-permute-start.7 = (bf16[2,2048,128]{2,1,0:T(8,128)(2,1)}, bf16[2,2048,128]{2,1,0:T(8,128)(2,1)}, u32[]{:S(2)}, u32[]{:S(2)}) collective-permute-start(bf16[2,2048,128]{2,1,0:T(8,128)(2,1)} %get-tuple-element.31.refs_0_), channel_id=1, source_target_pairs={{2,0},{4,2},{1,3},{6,4},{3,5},{8,6},{5,7},{10,8},{7,9},{12,10},{9,... | collective-permute-start | bytes 3145736 | tf_op jit(solution)/shard_map/ppermute | solution.py:404
  61.2 27.7 %collective-permute-start.10 = (bf16[2,2048,128]{2,1,0:T(8,128)(2,1)}, bf16[2,2048,128]{2,1,0:T(8,128)(2,1)}, u32[]{:S(2)}, u32[]{:S(2)}) collective-permute-start(bf16[2,2048,128]{2,1,0:T(8,128)(2,1)} %get-tuple-element.31.refs_0_), channel_id=1, source_target_pairs={{0,1},{1,0},{2,3},{3,2},{4,5},{5,4},{6,7},{7,6},{8,9},{9,8},{10,11... | collective-permute-start | bytes 3145736 | tf_op jit(solution)/shard_map/ppermute | solution.py:403
  63.9 43.6 %all-to-all-start.1 = ((bf16[16,3,2,64,128]{4,3,2,1,0:T(8,128)(2,1)}), bf16[16,3,2,64,128]{4,3,2,1,0:T(8,128)(2,1)S(1)}, u32[]{:S(2)}, u32[]{:S(2)}) async-start(bf16[16,3,2,64,128]{4,3,2,1,0:T(8,128)(2,1)} %split_spatial.2), calls=%async_computation.1 | async-start | bytes 3145728 | tf_op jit(solution)/shard_map/all_to_all | solution.py:397
  86.9 47.6 %collective-permute-start.8 = (bf16[2,2048,128]{2,1,0:T(8,128)(2,1)}, bf16[2,2048,128]{2,1,0:T(8,128)(2,1)}, u32[]{:S(2)}, u32[]{:S(2)}) collective-permute-start(bf16[2,2048,128]{2,1,0:T(8,128)(2,1)} %get-tuple-element.31.refs_0_), channel_id=1, source_target_pairs={{3,1},{0,2},{5,3},{2,4},{7,5},{4,6},{9,7},{6,8},{11,9},{8,10},{13,... | collective-permute-start | bytes 3145736 | tf_op jit(solution)/shard_map/ppermute | solution.py:406
  88.8 31.9 %collective-permute-start.9 = (bf16[2,2048,128]{2,1,0:T(8,128)(2,1)}, bf16[2,2048,128]{2,1,0:T(8,128)(2,1)}, u32[]{:S(2)}, u32[]{:S(2)}) collective-permute-start(bf16[2,2048,128]{2,1,0:T(8,128)(2,1)} %collective-permute-done.7.refs_0_), channel_id=1, source_target_pairs={{0,1},{1,0},{2,3},{3,2},{4,5},{5,4},{6,7},{7,6},{8,9},{9,8},{10,11... | collective-permute-start | bytes 3145736 | tf_op jit(solution)/shard_map/ppermute | solution.py:409
  88.9 13.9 %copy-start = (s32[4,8,8]{2,1,0:T(8,128)S(1)}, s32[4,8,8]{2,1,0:T(8,128)}, u32[]{:S(2)}) copy-start(s32[4,8,8]{2,1,0:T(8,128)} %mask_ref.3) | copy-start | bytes 3076
  88.9 13.9 %copy-start.1 = (s32[16]{0:T(128)S(1)}, s32[16]{0:T(128)}, u32[]{:S(2)}) copy-start(s32[16]{0:T(128)} %pattern_ref.3) | copy-start | bytes 196
  112.4 29.7 %all-to-all-start.3 = ((bf16[16,4,64,128]{3,2,1,0:T(8,128)(2,1)}), bf16[16,4,64,128]{3,2,1,0:T(8,128)(2,1)S(1)}, u32[]{:S(2)}, u32[]{:S(2)}) async-start(bf16[16,4,64,128]{3,2,1,0:T(8,128)(2,1)} %spatial.3), calls=%async_computation.3 | async-start | bytes 2097152 | tf_op jit(solution)/shard_map/all_to_all | solution.py:419
  142.0 15.9 %all-to-all-start = ((bf16[8,4,64,128]{3,2,1,0:T(8,128)(2,1)}), bf16[8,4,64,128]{3,2,1,0:T(8,128)(2,1)S(1)}, u32[]{:S(2)}, u32[]{:S(2)}) async-start(bf16[8,4,64,128]{3,2,1,0:T(8,128)(2,1)} %temporal_last.1), calls=%async_computation | async-start | bytes 1048576 | tf_op jit(solution)/shard_map/all_to_all | solution.py:416

commit v2 on v1

--- a/solution.py
+++ b/solution.py
@@ -149,7 +149,7 @@
     return (source >= 0) & (source < NS)
 
 
-def attend(q_ref, kv_ref, s_buf, state, done):
+def attend(q_ref, kv_ref, s_buf, state, ready, done):
     k = kv_ref[0]
     tiles = q_ref.shape[0] // QT
 
@@ -157,6 +157,7 @@
         return scores_of(q_ref[i * QT : (i + 1) * QT], k)
 
     s_buf[0] = raw(0)
+    ready()
     for i in range(tiles):
         if i + 1 < tiles:
             s_buf[(i + 1) % 2] = raw(i + 1)
@@ -174,62 +175,124 @@
         done(i, top, mixed)
 
 
-def temporal_kernel(offsets, resume, strip_ref, q_ref, *refs):
+def state_copies(sources, targets, sem, tile=None):
+    at = slice(0, sources[0].shape[0]) if tile is None else slice(tile * QT, (tile + 1) * QT)
+    first = 0 if tile is None else 2 * tile
+    return [
+        pltpu.make_async_copy(source.at[at], target.at[at], sem.at[first + n])
+        for n, (source, target) in enumerate(zip(sources, targets))
+    ]
+
+
+def first_kernel(q_ref, own_ref, partner_ref, top_out, mix_out, s_buf, top_ref, mix_ref, sem):
+    tiles = q_ref.shape[0] // QT
+    state = (top_ref, mix_ref)
+
+    def leave(i):
+        return state_copies(state, (top_out, mix_out), sem, i)
+
+    def keep(i, top, mixed):
+        at = slice(i * QT, (i + 1) * QT)
+        top_ref[at] = top
+        mix_ref[at] = mixed
+
+    def send(i, top, mixed):
+        keep(i, top, mixed)
+        for copy in leave(i):
+            copy.start()
+
+    attend(q_ref, own_ref, s_buf, None, lambda: None, keep)
+    attend(q_ref, partner_ref, s_buf, state, lambda: None, send)
+    for i in range(tiles):
+        for copy in leave(i):
+            copy.wait()
+
+
+def state_shapes(rows):
+    return [((rows, DH), F32), ((rows, 2 * DH), F32)]
+
+
+def temporal_cost(count, rows):
+    return pl.CostEstimate(
+        flops=count * rows**2 * DH * 8,
+        transcendentals=count * rows**2,
+        bytes_accessed=count * rows * DH * 4,
+    )
+
+
+def temporal_first(q, own, partner):
+    rows = q.shape[0]
+    shapes = state_shapes(rows)
+    return pl.pallas_call(
+        first_kernel,
+        in_specs=[whole()] * 3,
+        out_specs=[anywhere()] * 2,
+        out_shape=[pltpu.HBM(*shape) for shape in shapes],
+        scratch_shapes=[
+            pltpu.VMEM((2, QT, rows), F32),
+            *[pltpu.VMEM(*shape) for shape in shapes],
+            pltpu.SemaphoreType.DMA((2 * (rows // QT),)),
+        ],
+        compiler_params=params(24),
+        cost_estimate=temporal_cost(2, rows),
+        name="temporal_first",
+    )(in_hbm(q), in_vmem(own), in_vmem(partner))
+
+
+def middle_kernel(offsets, strip_ref, q_ref, *refs):
     count = len(offsets)
-    kv_refs, rest = refs[:count], refs[count:]
-    if resume:
-        old_top, old_mix, top_ref, mix_ref, s_buf, sem = rest
-        loads = [
-            pltpu.make_async_copy(old_top, top_ref, sem.at[0]),
-            pltpu.make_async_copy(old_mix, mix_ref, sem.at[1]),
-        ]
-        for load in loads:
-            load.start()
+    kv_refs, (old_top, old_mix, top_ref, mix_ref, s_buf, kv_buf, sem) = refs[:count], refs[count:]
+    loads = state_copies((old_top, old_mix), (top_ref, mix_ref), sem)
+    for load in loads:
+        load.start()
+
+    def arrive():
         for load in loads:
             load.wait()
-    else:
-        top_ref, mix_ref, s_buf = rest
 
     def done(i, top, mixed):
         at = slice(i * QT, (i + 1) * QT)
         top_ref[at] = top
         mix_ref[at] = mixed
 
-    for offset, kv_ref in zip(offsets, kv_refs):
-        if offset == 0:
-            attend(q_ref, kv_ref, s_buf, None, done)
-        else:
-            pl.when(usable(strip_ref, offset))(
-                lambda kv_ref=kv_ref: attend(q_ref, kv_ref, s_buf, (top_ref, mix_ref), done)
-            )
-
-
-def temporal(strip, q, strips, state=None):
+    def strip(index, carry):
+        valid = False
+        for i in range(count):
+            here = index == i
+
+            @pl.when(here)
+            def _(i=i):
+                kv_buf[...] = kv_refs[i][...]
+
+            valid = valid | (here & usable(strip_ref, offsets[i]))
+
+        def ready():
+            pl.when(index == 0)(arrive)
+
+        pl.when(valid)(lambda: attend(q_ref, kv_buf, s_buf, (top_ref, mix_ref), ready, done))
+        pl.when((index == 0) & jnp.logical_not(valid))(arrive)
+        return carry
+
+    lax.fori_loop(0, count, strip, 0)
+
+
+def temporal_middle(strip, q, strips, state):
     rows = q.shape[0]
     count = len(strips)
-    state_shape = [((rows, DH), F32), ((rows, 2 * DH), F32)]
-    args = [strip, in_hbm(q), *[in_vmem(x) for x in strips.values()]]
-    in_specs = [scalars()] + [whole()] * (1 + count)
-    scratch = [pltpu.VMEM((2, QT, rows), F32)]
-    if state is not None:
-        args += [in_hbm(x) for x in state]
-        in_specs += [anywhere()] * 2
-        scratch.append(pltpu.SemaphoreType.DMA((2,)))
-    space = pltpu.HBM if state is None else pltpu.VMEM
-    cost = pl.CostEstimate(
-        flops=count * rows**2 * DH * 8,
-        transcendentals=count * rows**2,
-        bytes_accessed=count * rows * DH * 4,
-    )
-    return pl.pallas_call(
-        functools.partial(temporal_kernel, tuple(strips), state is not None),
-        in_specs=in_specs,
+    return pl.pallas_call(
+        functools.partial(middle_kernel, tuple(strips)),
+        in_specs=[scalars(), *[whole()] * (1 + count), *[anywhere()] * 2],
         out_specs=[whole()] * 2,
-        out_shape=[space(*shape) for shape in state_shape],
-        scratch_shapes=scratch,
+        out_shape=[pltpu.VMEM(*shape) for shape in state_shapes(rows)],
+        scratch_shapes=[
+            pltpu.VMEM((2, QT, rows), F32),
+            pltpu.VMEM((2, rows, DH), BF16),
+            pltpu.SemaphoreType.DMA((2,)),
+        ],
         compiler_params=params(20),
-        cost_estimate=cost,
-    )(*args)
+        cost_estimate=temporal_cost(count, rows),
+        name="temporal_middle",
+    )(strip, in_hbm(q), *[in_vmem(x) for x in strips.values()], *[in_hbm(x) for x in state])
 
 
 def temporal_last_kernel(offset, strip_ref, group_ref, q_ref, kv_ref, top_ref, mix_ref, *rest):
@@ -245,7 +308,9 @@
             out_ref[target] = result.reshape(out_ref.shape[1:])
 
     valid = usable(strip_ref, offset)
-    pl.when(valid)(lambda: attend(q_ref, kv_ref, s_buf, (top_ref, mix_ref), done))
+    pl.when(valid)(
+        lambda: attend(q_ref, kv_ref, s_buf, (top_ref, mix_ref), lambda: None, done)
+    )
 
     @pl.when(jnp.logical_not(valid))
     def _():
@@ -262,9 +327,7 @@
         out_shape=pltpu.HBM(shape, BF16),
         scratch_shapes=[pltpu.VMEM((2, QT, rows), F32)],
         compiler_params=params(20),
-        cost_estimate=pl.CostEstimate(
-            flops=rows**2 * DH * 8, transcendentals=rows**2, bytes_accessed=rows * DH * 4
-        ),
+        cost_estimate=temporal_cost(1, rows),
         name="temporal_last",
     )(strip, group, in_hbm(q), *[in_vmem(x) for x in (kv, *state)])
 
@@ -392,7 +455,10 @@
     qkv_a = split_spatial(0, half, queries, keys, values)
     qkv_a = lax.all_to_all(qkv_a, "strip", split_axis=0, concat_axis=0, tiled=True)
     slabs = split_temporal(group_arg, queries, keys, values)
-    slabs = [slabs[0]] + [paired(slabs[d], d) for d in range(1, NF)]
+    moved = {0: slabs[0]}
+    moved.update({d: paired(slabs[d], d) for d in range(1, NF, 2)})
+    moved.update({d: paired(slabs[d], d) for d in range(2, NF, 2)})
+    slabs = [moved[d] for d in range(NF)]
     qkv_b = split_spatial(half, half, queries, keys, values)
     qkv_b = lax.all_to_all(qkv_b, "strip", split_axis=0, concat_axis=0, tiled=True)
     t_q, own = collect(slabs)
@@ -408,8 +474,8 @@
     )
     passed = lax.ppermute(shared, "strip", swap)
 
-    state = temporal(strip_arg, t_q, {0: own, 1: partner})
-    state = temporal(strip_arg, t_q, {2: shared, -1: passed}, state)
+    state = temporal_first(t_q, own, partner)
+    state = temporal_middle(strip_arg, t_q, {2: shared, -1: passed}, state)
     t_out = temporal_last(
         strip_arg, group_arg, t_q, -2, single, state, (NF, frames, spots, DH)
     )

time: 161 us -> 160 us (level)
  no operation moved by 1% of the time
where the time goes in v2:
time: 160 us; the launch traced here: 158 us
  waiting for transfers between devices  59.5 us (37%)
  Pallas kernels  53.7 us (34%)
  starting transfers between devices  44.7 us (28%)
    ppermute x7, waiting for transfers between devices, paired(): return lax.ppermute(block, 'frame', [(i, i ^ slot) for i in range(NF)])  30.6 us
    ppermute x1, waiting for transfers between devices, main(): lax.ppermute(own, 'strip', [(s, i) for i, s in enumerate(shared_from) if...  18.8 us
    ppermute x7, starting transfers between devices, paired(): return lax.ppermute(block, 'frame', [(i, i ^ slot) for i in range(NF)])  14.2 us
    pallas_call x1, Pallas kernels, temporal_middle(): pl.pallas_call(functools.partial(middle_kernel, tuple(strips)), in_specs=...  13.6 us
    pallas_call x1, Pallas kernels, temporal_first(): pl.pallas_call(first_kernel, in_specs=[whole()] * 3, out_specs=[anywhere(...  12.8 us
    all_to_all x1, waiting for transfers between devices, main(): lax.all_to_all(t_out, 'frame', split_axis=0, concat_axis=0, tiled=True)  10.1 us
    pallas_call x2, Pallas kernels, spatial(): pl.pallas_call(functools.partial(spatial_kernel, first), in_specs=[*[scal...  9.79 us
    all_to_all x1, starting transfers between devices, main(): lax.all_to_all(s_out, 'strip', split_axis=0, concat_axis=0, tiled=True)  8.33 us
  transfers between devices with their start and end apart: 15, of which 5 were waited for; matrix products, arithmetic and copies ran while one was open for 0% of the time, Pallas kernels for 32%

profile of v2, /device:TPU:32, one launch (start us, length us, event | category | flops | bytes accessed | tf_op | source)
XLA Modules:
  0.0 158.2 jit_solution(15822255069152580737)
XLA Ops:
  0.0 2.6 %split_spatial.3 = bf16[16,3,2,64,128]{4,3,2,1,0:T(8,128)(2,1)} custom-call(bf16[4,64,3072]{2,1,0:T(8,128)(2,1)} %q_ref.5, bf16[4,64,3072]{2,1,0:T(8,128)(2,1)} %k_ref.5, bf16[4,64,3072]{2,1,0:T(8,128)(2,1)} %v_ref.5), custom_call_target="tpu_custom_call" | custom-call | tf_op jit(solution)/shard_map/split_spatial/pallas_call | solution.py:74
  2.6 5.8 %all-to-all-start.2 = ((bf16[16,3,2,64,128]{4,3,2,1,0:T(8,128)(2,1)}), bf16[16,3,2,64,128]{4,3,2,1,0:T(8,128)(2,1)S(1)}, u32[]{:S(2)}, u32[]{:S(2)}) async-start(bf16[16,3,2,64,128]{4,3,2,1,0:T(8,128)(2,1)} %split_spatial.3), calls=%async_computation.2 | async-start | bytes 3145728 | tf_op jit(solution)/shard_map/all_to_all | solution.py:456
  8.4 1.5 split_temporal.1
  10.0 3.1 %collective-permute-start = (bf16[3,4,64,128]{3,2,1,0:T(8,128)(2,1)S(1)}, bf16[3,4,64,128]{3,2,1,0:T(8,128)(2,1)S(1)}, u32[]{:S(2)}, u32[]{:S(2)}) collective-permute-start(bf16[3,4,64,128]{3,2,1,0:T(8,128)(2,1)S(1)} %get-tuple-element.22), channel_id=1, source_target_pairs={{0,16},{16,0},{32,48},{48,32},{64,80},{80,64},{96,112},{112,96},{1... | collective-permute-start | bytes 589832 | tf_op jit(solution)/shard_map/ppermute | solution.py:444
  13.0 1.6 collective-permute-start.1
  15.0 3.2 %collective-permute-start.3 = (bf16[3,4,64,128]{3,2,1,0:T(8,128)(2,1)S(1)}, bf16[3,4,64,128]{3,2,1,0:T(8,128)(2,1)S(1)}, u32[]{:S(2)}, u32[]{:S(2)}) collective-permute-start(bf16[3,4,64,128]{3,2,1,0:T(8,128)(2,1)S(1)} %get-tuple-element.25), channel_id=1, source_target_pairs={{0,64},{16,80},{32,96},{48,112},{64,0},{80,16},{96,32},{112,48},{1... | collective-permute-start | bytes 589832 | tf_op jit(solution)/shard_map/ppermute | solution.py:444
  18.2 2.7 %collective-permute-start.4 = (bf16[3,4,64,128]{3,2,1,0:T(8,128)(2,1)S(1)}, bf16[3,4,64,128]{3,2,1,0:T(8,128)(2,1)S(1)}, u32[]{:S(2)}, u32[]{:S(2)}) collective-permute-start(bf16[3,4,64,128]{3,2,1,0:T(8,128)(2,1)S(1)} %get-tuple-element.26), channel_id=1, source_target_pairs={{0,80},{16,64},{32,112},{48,96},{64,16},{80,0},{96,48},{112,32},{1... | collective-permute-start | bytes 589832 | tf_op jit(solution)/shard_map/ppermute | solution.py:444
  21.0 21.1 %collective-permute-done.refs_1_ = bf16[3,4,64,128]{3,2,1,0:T(8,128)(2,1)S(1)} collective-permute-done((bf16[3,4,64,128]{3,2,1,0:T(8,128)(2,1)S(1)}, bf16[3,4,64,128]{3,2,1,0:T(8,128)(2,1)S(1)}, u32[]{:S(2)}, u32[]{:S(2)}) %collective-permute-start) | collective-permute-done | bytes 196640 | tf_op jit(solution)/shard_map/ppermute | solution.py:444
  42.1 3.0 %collective-permute-start.5 = (bf16[3,4,64,128]{3,2,1,0:T(8,128)(2,1)S(1)}, bf16[3,4,64,128]{3,2,1,0:T(8,128)(2,1)S(1)}, u32[]{:S(2)}, u32[]{:S(2)}) collective-permute-start(bf16[3,4,64,128]{3,2,1,0:T(8,128)(2,1)S(1)} %get-tuple-element.27), channel_id=1, source_target_pairs={{0,96},{16,112},{32,64},{48,80},{64,32},{80,48},{96,0},{112,16},{1... | collective-permute-start | bytes 589832 | tf_op jit(solution)/shard_map/ppermute | solution.py:444
  45.3 5.7 %collective-permute-done.5.refs_6_ = bf16[3,4,64,128]{3,2,1,0:T(8,128)(2,1)S(1)} collective-permute-done((bf16[3,4,64,128]{3,2,1,0:T(8,128)(2,1)S(1)}, bf16[3,4,64,128]{3,2,1,0:T(8,128)(2,1)S(1)}, u32[]{:S(2)}, u32[]{:S(2)}) %collective-permute-start.5) | collective-permute-done | bytes 196640 | tf_op jit(solution)/shard_map/ppermute | solution.py:444
  51.0 3.7 %collective-permute-done.6.refs_7_ = bf16[3,4,64,128]{3,2,1,0:T(8,128)(2,1)S(1)} collective-permute-done((bf16[3,4,64,128]{3,2,1,0:T(8,128)(2,1)S(1)}, bf16[3,4,64,128]{3,2,1,0:T(8,128)(2,1)S(1)}, u32[]{:S(2)}, u32[]{:S(2)}) %collective-permute-start.6) | collective-permute-done | bytes 196640 | tf_op jit(solution)/shard_map/ppermute | solution.py:444
  56.0 5.2 %collective-permute-start.7 = (bf16[2,2048,128]{2,1,0:T(8,128)(2,1)}, bf16[2,2048,128]{2,1,0:T(8,128)(2,1)}, u32[]{:S(2)}, u32[]{:S(2)}) collective-permute-start(bf16[2,2048,128]{2,1,0:T(8,128)(2,1)} %get-tuple-element.31.own_ref), channel_id=1, source_target_pairs={{2,0},{4,2},{1,3},{6,4},{3,5},{8,6},{5,7},{10,8},{7,9},{12,10},{9,... | collective-permute-start | bytes 3145736 | tf_op jit(solution)/shard_map/ppermute | solution.py:470
  61.3 2.6 %split_spatial.2 = bf16[16,3,2,64,128]{4,3,2,1,0:T(8,128)(2,1)} custom-call(bf16[4,64,3072]{2,1,0:T(8,128)(2,1)} %q_ref.5, bf16[4,64,3072]{2,1,0:T(8,128)(2,1)} %k_ref.5, bf16[4,64,3072]{2,1,0:T(8,128)(2,1)} %v_ref.5), custom_call_target="tpu_custom_call" | custom-call | tf_op jit(solution)/shard_map/split_spatial/pallas_call | solution.py:74
  63.9 4.1 %all-to-all-start.1 = ((bf16[16,3,2,64,128]{4,3,2,1,0:T(8,128)(2,1)}), bf16[16,3,2,64,128]{4,3,2,1,0:T(8,128)(2,1)S(1)}, u32[]{:S(2)}, u32[]{:S(2)}) async-start(bf16[16,3,2,64,128]{4,3,2,1,0:T(8,128)(2,1)} %split_spatial.2), calls=%async_computation.1 | async-start | bytes 3145728 | tf_op jit(solution)/shard_map/all_to_all | solution.py:463
  68.0 18.8 %collective-permute-done.7.refs_0_ = bf16[2,2048,128]{2,1,0:T(8,128)(2,1)} collective-permute-done((bf16[2,2048,128]{2,1,0:T(8,128)(2,1)}, bf16[2,2048,128]{2,1,0:T(8,128)(2,1)}, u32[]{:S(2)}, u32[]{:S(2)}) %collective-permute-start.7) | collective-permute-done | bytes 1048608 | tf_op jit(solution)/shard_map/ppermute | solution.py:470
  86.9 1.9 %collective-permute-start.8 = (bf16[2,2048,128]{2,1,0:T(8,128)(2,1)}, bf16[2,2048,128]{2,1,0:T(8,128)(2,1)}, u32[]{:S(2)}, u32[]{:S(2)}) collective-permute-start(bf16[2,2048,128]{2,1,0:T(8,128)(2,1)} %get-tuple-element.31.own_ref), channel_id=1, source_target_pairs={{3,1},{0,2},{5,3},{2,4},{7,5},{4,6},{9,7},{6,8},{11,9},{8,10},{13,... | collective-permute-start | bytes 3145736 | tf_op jit(solution)/shard_map/ppermute | solution.py:472
  89.1 12.8 %temporal_first.1 = (f32[2048,128]{1,0:T(8,128)}, f32[2048,256]{1,0:T(8,128)}) custom-call(bf16[2048,128]{1,0:T(8,128)(2,1)} %get-tuple-element.29.q_ref, bf16[2,2048,128]{2,1,0:T(8,128)(2,1)} %get-tuple-element.31.own_ref, bf16[2,2048,128]{2,1,0:T(8,128)(2,1)} %collective-permute-done.10.partner_ref), custom_call_target="tpu_custom_call" | custom-call | flops 8589934592 | bytes 2097152 | tf_op jit(solution)/shard_map/temporal_first/pallas_call | solution.py:226
  102.0 5.0 %spatial.2.rest_0_ = bf16[16,4,64,128]{3,2,1,0:T(8,128)(2,1)} custom-call(s32[1]{0:T(128)} %bitcast.strip_ref, s32[16]{0:T(128)S(1)} %copy-done.1, s32[4,8,8]{2,1,0:T(8,128)S(1)} %copy-done, bf16[16,3,2,64,128]{4,3,2,1,0:T(8,128)(2,1)S(1)} %all-to-all-done.2.qkv_ref), custom_call_target="tpu_custom_call" | custom-call | flops 2147483648 | bytes 2097152 | tf_op jit(solution)/shard_map/spatial/pallas_call | solution.py:396
  107.0 4.8 %spatial.3 = bf16[16,4,64,128]{3,2,1,0:T(8,128)(2,1)} custom-call(s32[1]{0:T(128)} %bitcast.strip_ref, s32[16]{0:T(128)S(1)} %copy-done.1, s32[4,8,8]{2,1,0:T(8,128)S(1)} %copy-done, bf16[16,3,2,64,128]{4,3,2,1,0:T(8,128)(2,1)S(1)} %all-to-all-done.1.qkv_ref, bf16[16,4,64,128]{3,2,1,0:T(8,128)(2,1)} %spatial.2.rest_0_), custom_call_target="tpu_custom_call", output_to_operand_aliasing={{}: (4, {})} | custom-call | flops 2147483648 | bytes 2097152 | tf_op jit(solution)/shard_map/spatial/pallas_call | solution.py:396
  111.8 8.3 %all-to-all-start.3 = ((bf16[16,4,64,128]{3,2,1,0:T(8,128)(2,1)}), bf16[16,4,64,128]{3,2,1,0:T(8,128)(2,1)S(1)}, u32[]{:S(2)}, u32[]{:S(2)}) async-start(bf16[16,4,64,128]{3,2,1,0:T(8,128)(2,1)} %spatial.3), calls=%async_computation.3 | async-start | bytes 2097152 | tf_op jit(solution)/shard_map/all_to_all | solution.py:485
  120.1 13.6 %temporal_middle.1 = (f32[2048,128]{1,0:T(8,128)S(1)}, f32[2048,256]{1,0:T(8,128)S(1)}) custom-call(s32[1]{0:T(128)} %bitcast.strip_ref, bf16[2048,128]{1,0:T(8,128)(2,1)} %get-tuple-element.29.q_ref, bf16[2,2048,128]{2,1,0:T(8,128)(2,1)} %collective-permute-done.7.refs_0_, bf16[2,2048,128]{2,1,0:T(8,128)(2,1)} %collective-permute-done.9.refs_1_, ...), custom_call_target="tpu_custom_call" | custom-call | flops 8589934592 | bytes 2097152 | tf_op jit(solution)/shard_map/temporal_middle/pallas_call | solution.py:282
  133.7 7.5 %temporal_last.1 = bf16[8,4,64,128]{3,2,1,0:T(8,128)(2,1)} custom-call(s32[1]{0:T(128)} %bitcast.strip_ref, s32[1]{0:T(128)} %bitcast.1.group_ref, bf16[2048,128]{1,0:T(8,128)(2,1)} %get-tuple-element.29.q_ref, bf16[2,2048,128]{2,1,0:T(8,128)(2,1)} %collective-permute-done.8.kv_ref, f32[2048,128]{1,0:T(8,128)S(1)} %get-tuple-element.35.top_ref, ...), custom_call_target="tpu_custom_call" | custom-call | flops 4294967296 | bytes 1048576 | tf_op jit(solution)/shard_map/temporal_last/pallas_call | solution.py:323
  141.3 4.8 %all-to-all-start = ((bf16[8,4,64,128]{3,2,1,0:T(8,128)(2,1)}), bf16[8,4,64,128]{3,2,1,0:T(8,128)(2,1)S(1)}, u32[]{:S(2)}, u32[]{:S(2)}) async-start(bf16[8,4,64,128]{3,2,1,0:T(8,128)(2,1)} %temporal_last.1), calls=%async_computation | async-start | bytes 1048576 | tf_op jit(solution)/shard_map/all_to_all | solution.py:482
  147.1 10.1 %all-to-all-done.refs_0_ = bf16[8,4,64,128]{3,2,1,0:T(8,128)(2,1)S(1)} async-done(((bf16[8,4,64,128]{3,2,1,0:T(8,128)(2,1)}), bf16[8,4,64,128]{3,2,1,0:T(8,128)(2,1)S(1)}, u32[]{:S(2)}, u32[]{:S(2)}) %all-to-all-start) | async-done | bytes 524320 | tf_op jit(solution)/shard_map/all_to_all | solution.py:482
  (21 shorter events, 4.2 us)
Async XLA Ops:
  2.6 61.3 %all-to-all-start.2 = ((bf16[16,3,2,64,128]{4,3,2,1,0:T(8,128)(2,1)}), bf16[16,3,2,64,128]{4,3,2,1,0:T(8,128)(2,1)S(1)}, u32[]{:S(2)}, u32[]{:S(2)}) async-start(bf16[16,3,2,64,128]{4,3,2,1,0:T(8,128)(2,1)} %split_spatial.3), calls=%async_computation.2 | async-start | bytes 3145728 | tf_op jit(solution)/shard_map/all_to_all | solution.py:456
  10.0 32.1 %collective-permute-start = (bf16[3,4,64,128]{3,2,1,0:T(8,128)(2,1)S(1)}, bf16[3,4,64,128]{3,2,1,0:T(8,128)(2,1)S(1)}, u32[]{:S(2)}, u32[]{:S(2)}) collective-permute-start(bf16[3,4,64,128]{3,2,1,0:T(8,128)(2,1)S(1)} %get-tuple-element.22), channel_id=1, source_target_pairs={{0,16},{16,0},{32,48},{48,32},{64,80},{80,64},{96,112},{112,96},{1... | collective-permute-start | bytes 589832 | tf_op jit(solution)/shard_map/ppermute | solution.py:444
  13.0 32.1 %collective-permute-start.1 = (bf16[3,4,64,128]{3,2,1,0:T(8,128)(2,1)S(1)}, bf16[3,4,64,128]{3,2,1,0:T(8,128)(2,1)S(1)}, u32[]{:S(2)}, u32[]{:S(2)}) collective-permute-start(bf16[3,4,64,128]{3,2,1,0:T(8,128)(2,1)S(1)} %get-tuple-element.23), channel_id=1, source_target_pairs={{0,32},{16,48},{32,0},{48,16},{64,96},{80,112},{96,64},{112,80},{1... | collective-permute-start | bytes 589832 | tf_op jit(solution)/shard_map/ppermute | solution.py:444
  14.6 30.7 %collective-permute-start.2 = (bf16[3,4,64,128]{3,2,1,0:T(8,128)(2,1)S(1)}, bf16[3,4,64,128]{3,2,1,0:T(8,128)(2,1)S(1)}, u32[]{:S(2)}, u32[]{:S(2)}) collective-permute-start(bf16[3,4,64,128]{3,2,1,0:T(8,128)(2,1)S(1)} %get-tuple-element.24), channel_id=1, source_target_pairs={{0,48},{16,32},{32,16},{48,0},{64,112},{80,96},{96,80},{112,64},{1... | collective-permute-start | bytes 589832 | tf_op jit(solution)/shard_map/ppermute | solution.py:444
  15.0 30.3 %collective-permute-start.3 = (bf16[3,4,64,128]{3,2,1,0:T(8,128)(2,1)S(1)}, bf16[3,4,64,128]{3,2,1,0:T(8,128)(2,1)S(1)}, u32[]{:S(2)}, u32[]{:S(2)}) collective-permute-start(bf16[3,4,64,128]{3,2,1,0:T(8,128)(2,1)S(1)} %get-tuple-element.25), channel_id=1, source_target_pairs={{0,64},{16,80},{32,96},{48,112},{64,0},{80,16},{96,32},{112,48},{1... | collective-permute-start | bytes 589832 | tf_op jit(solution)/shard_map/ppermute | solution.py:444
  18.2 27.1 %collective-permute-start.4 = (bf16[3,4,64,128]{3,2,1,0:T(8,128)(2,1)S(1)}, bf16[3,4,64,128]{3,2,1,0:T(8,128)(2,1)S(1)}, u32[]{:S(2)}, u32[]{:S(2)}) collective-permute-start(bf16[3,4,64,128]{3,2,1,0:T(8,128)(2,1)S(1)} %get-tuple-element.26), channel_id=1, source_target_pairs={{0,80},{16,64},{32,112},{48,96},{64,16},{80,0},{96,48},{112,32},{1... | collective-permute-start | bytes 589832 | tf_op jit(solution)/shard_map/ppermute | solution.py:444
  42.1 9.0 %collective-permute-start.5 = (bf16[3,4,64,128]{3,2,1,0:T(8,128)(2,1)S(1)}, bf16[3,4,64,128]{3,2,1,0:T(8,128)(2,1)S(1)}, u32[]{:S(2)}, u32[]{:S(2)}) collective-permute-start(bf16[3,4,64,128]{3,2,1,0:T(8,128)(2,1)S(1)} %get-tuple-element.27), channel_id=1, source_target_pairs={{0,96},{16,112},{32,64},{48,80},{64,32},{80,48},{96,0},{112,16},{1... | collective-permute-start | bytes 589832 | tf_op jit(solution)/shard_map/ppermute | solution.py:444
  45.1 9.7 %collective-permute-start.6 = (bf16[3,4,64,128]{3,2,1,0:T(8,128)(2,1)S(1)}, bf16[3,4,64,128]{3,2,1,0:T(8,128)(2,1)S(1)}, u32[]{:S(2)}, u32[]{:S(2)}) collective-permute-start(bf16[3,4,64,128]{3,2,1,0:T(8,128)(2,1)S(1)} %get-tuple-element.28), channel_id=1, source_target_pairs={{0,112},{16,96},{32,80},{48,64},{64,48},{80,32},{96,16},{112,0},{1... | collective-permute-start | bytes 589832 | tf_op jit(solution)/shard_map/ppermute | solution.py:444
  56.0 30.8 %collective-permute-start.7 = (bf16[2,2048,128]{2,1,0:T(8,128)(2,1)}, bf16[2,2048,128]{2,1,0:T(8,128)(2,1)}, u32[]{:S(2)}, u32[]{:S(2)}) collective-permute-start(bf16[2,2048,128]{2,1,0:T(8,128)(2,1)} %get-tuple-element.31.own_ref), channel_id=1, source_target_pairs={{2,0},{4,2},{1,3},{6,4},{3,5},{8,6},{5,7},{10,8},{7,9},{12,10},{9,... | collective-permute-start | bytes 3145736 | tf_op jit(solution)/shard_map/ppermute | solution.py:470
  61.2 27.9 %collective-permute-start.10 = (bf16[2,2048,128]{2,1,0:T(8,128)(2,1)}, bf16[2,2048,128]{2,1,0:T(8,128)(2,1)}, u32[]{:S(2)}, u32[]{:S(2)}) collective-permute-start(bf16[2,2048,128]{2,1,0:T(8,128)(2,1)} %get-tuple-element.31.own_ref), channel_id=1, source_target_pairs={{0,1},{1,0},{2,3},{3,2},{4,5},{5,4},{6,7},{7,6},{8,9},{9,8},{10,11... | collective-permute-start | bytes 3145736 | tf_op jit(solution)/shard_map/ppermute | solution.py:469
  63.9 43.0 %all-to-all-start.1 = ((bf16[16,3,2,64,128]{4,3,2,1,0:T(8,128)(2,1)}), bf16[16,3,2,64,128]{4,3,2,1,0:T(8,128)(2,1)S(1)}, u32[]{:S(2)}, u32[]{:S(2)}) async-start(bf16[16,3,2,64,128]{4,3,2,1,0:T(8,128)(2,1)} %split_spatial.2), calls=%async_computation.1 | async-start | bytes 3145728 | tf_op jit(solution)/shard_map/all_to_all | solution.py:463
  86.9 46.9 %collective-permute-start.8 = (bf16[2,2048,128]{2,1,0:T(8,128)(2,1)}, bf16[2,2048,128]{2,1,0:T(8,128)(2,1)}, u32[]{:S(2)}, u32[]{:S(2)}) collective-permute-start(bf16[2,2048,128]{2,1,0:T(8,128)(2,1)} %get-tuple-element.31.own_ref), channel_id=1, source_target_pairs={{3,1},{0,2},{5,3},{2,4},{7,5},{4,6},{9,7},{6,8},{11,9},{8,10},{13,... | collective-permute-start | bytes 3145736 | tf_op jit(solution)/shard_map/ppermute | solution.py:472
  88.8 31.3 %collective-permute-start.9 = (bf16[2,2048,128]{2,1,0:T(8,128)(2,1)}, bf16[2,2048,128]{2,1,0:T(8,128)(2,1)}, u32[]{:S(2)}, u32[]{:S(2)}) collective-permute-start(bf16[2,2048,128]{2,1,0:T(8,128)(2,1)} %collective-permute-done.7.refs_0_), channel_id=1, source_target_pairs={{0,1},{1,0},{2,3},{3,2},{4,5},{5,4},{6,7},{7,6},{8,9},{9,8},{10,11... | collective-permute-start | bytes 3145736 | tf_op jit(solution)/shard_map/ppermute | solution.py:475
  89.1 12.9 %copy-start = (s32[4,8,8]{2,1,0:T(8,128)S(1)}, s32[4,8,8]{2,1,0:T(8,128)}, u32[]{:S(2)}) copy-start(s32[4,8,8]{2,1,0:T(8,128)} %mask_ref.3) | copy-start | bytes 3076
  89.1 12.9 %copy-start.1 = (s32[16]{0:T(128)S(1)}, s32[16]{0:T(128)}, u32[]{:S(2)}) copy-start(s32[16]{0:T(128)} %pattern_ref.3) | copy-start | bytes 196
  111.8 29.5 %all-to-all-start.3 = ((bf16[16,4,64,128]{3,2,1,0:T(8,128)(2,1)}), bf16[16,4,64,128]{3,2,1,0:T(8,128)(2,1)S(1)}, u32[]{:S(2)}, u32[]{:S(2)}) async-start(bf16[16,4,64,128]{3,2,1,0:T(8,128)(2,1)} %spatial.3), calls=%async_computation.3 | async-start | bytes 2097152 | tf_op jit(solution)/shard_map/all_to_all | solution.py:485
  141.3 15.9 %all-to-all-start = ((bf16[8,4,64,128]{3,2,1,0:T(8,128)(2,1)}), bf16[8,4,64,128]{3,2,1,0:T(8,128)(2,1)S(1)}, u32[]{:S(2)}, u32[]{:S(2)}) async-start(bf16[8,4,64,128]{3,2,1,0:T(8,128)(2,1)} %temporal_last.1), calls=%async_computation | async-start | bytes 1048576 | tf_op jit(solution)/shard_map/all_to_all | solution.py:482
